TPU v7x, 256 devices: a whole 4x4x8 slice. The times are simulated.
256 devices in a mesh: ctx: 8 (over y_hi, x), ch: 32 (over y_lo, z, core).
Axes of the slice: x: 4, y: 4 (y_hi: 2, y_lo: 2; y = y_hi * 2 + y_lo), z: 8, core: 2. Of those that a mesh axis runs over, the one named last changes fastest.
Arguments:
- conv_input: bfloat16 [8192, 4096], P('ch', 'ctx'), may hold values from -0.03125 to 0.03125
- output_grad: bfloat16 [8192, 4096], P('ch', 'ctx'), may hold values from -6 to 6
- long_filter: bfloat16 [128, 4096], P(None, 'ctx'), may hold values from -0.09375 to 0.09375
Outputs:
- input_grad: bfloat16 [8192, 4096], P('ch', 'ctx')
- filter_grad: float32 [128, 4096], P(None, 'ctx')
All inputs are finite; a program needn't handle non-finite values.
Results may differ from a plain program's by a relative error of at most 0.001.
Values may be sent and summed in bfloat16 or wider, within the bound.
No kernel may reach another device: no remote copies, remote signals or barrier semaphores. Data moves between devices by JAX's collectives and lax.ppermute only.
A program may use at most 128 MiB of HBM per device.

v0:
```python
import jax
import jax.numpy as jnp
from jax import lax
from jax.sharding import PartitionSpec as P

C = 8192
G = 128
TILE = 128


def toeplitz_table(filter_lags, total_tiles):
    groups = filter_lags.shape[0]
    taps_padded = jnp.pad(filter_lags, ((0, 0), (TILE, TILE)))
    blocks = taps_padded.reshape(groups, total_tiles + 2, TILE)
    windows = jnp.concatenate([blocks[:, :total_tiles], blocks[:, 1 : total_tiles + 1]], axis=2)
    reversed_windows = jnp.flip(windows, axis=2)
    repeated = jnp.broadcast_to(
        reversed_windows[:, :, None, :], (groups, total_tiles, TILE, 2 * TILE)
    )
    flat = repeated.reshape(groups, total_tiles, 2 * TILE * TILE)[:, :, : TILE * (2 * TILE - 1)]
    slanted = flat.reshape(groups, total_tiles, TILE, 2 * TILE - 1)
    return slanted[:, :, :, TILE - 1 : 2 * TILE - 1]


def lag_profile(lag_acc, total_tiles):
    groups = lag_acc.shape[0]
    slots = lag_acc.shape[1]
    flat = lag_acc.reshape(groups * slots, TILE, TILE)
    widened = jnp.pad(flat, ((0, 0), (0, 0), (TILE, 0))).reshape(groups * slots, 2 * TILE * TILE)
    widened = jnp.pad(widened, ((0, 0), (0, TILE)))
    slanted = widened.reshape(groups * slots, TILE, 2 * TILE + 1)
    totals = jnp.sum(slanted, axis=1).reshape(groups, slots, 2 * TILE + 1)
    upper = totals[:, :total_tiles, TILE : 2 * TILE]
    lower = totals[:, 1 : total_tiles + 1, 0:TILE]
    return (upper + lower).reshape(groups, total_tiles * TILE)


def contribute(own_block, incoming, tile_gap, table, lag_acc):
    own_tiles = own_block.shape[2]
    piece_tiles = incoming.shape[2]
    padded = jnp.pad(incoming, ((0, 0), (0, 0), (own_tiles - 1, own_tiles - 1), (0, 0)))

    def one_turn(turn, carried):
        grad_sum, acc_now = carried
        window = lax.dynamic_slice_in_dim(padded, turn, own_tiles, 2)
        offset_tiles = tile_gap + turn - (own_tiles - 1)
        tiles = lax.dynamic_index_in_dim(table, offset_tiles, 1, keepdims=False)
        grad_sum = grad_sum + jnp.einsum(
            "gcav,gvu->gcau", window, tiles, preferred_element_type=jnp.float32
        )
        cross = jnp.einsum("gcau,gcav->guv", own_block, window, preferred_element_type=jnp.float32)
        current = lax.dynamic_index_in_dim(acc_now, offset_tiles, 1, keepdims=True)
        acc_now = lax.dynamic_update_slice_in_dim(
            acc_now, current + cross[:, None], offset_tiles, 1
        )
        return (grad_sum, acc_now)

    first_turn = jnp.maximum(0, own_tiles - 1 - tile_gap)
    last_turn = own_tiles + piece_tiles - 1
    zero_grads = jnp.zeros(own_block.shape, jnp.float32)
    return lax.fori_loop(first_turn, last_turn, one_turn, (zero_grads, lag_acc))


def per_device(conv_input, output_grad, long_filter):
    channels, own_length = conv_input.shape
    group_size = C // G
    groups_here = max(1, channels // group_size)
    per_group = min(channels, group_size)
    own_tiles = own_length // TILE
    cycle_size = lax.axis_size("ctx")
    ctx_index = lax.axis_index("ctx")
    total_tiles = cycle_size * own_tiles
    first_group = lax.axis_index("ch") * channels // group_size
    filter_part = lax.dynamic_slice_in_dim(long_filter, first_group, groups_here, 0)
    filter_lags = lax.all_gather(filter_part, "ctx", axis=1, tiled=True)
    table = toeplitz_table(filter_lags, total_tiles)
    own_block = conv_input.reshape(groups_here, per_group, own_tiles, TILE)
    own_tile = ctx_index * own_tiles

    def add_piece(carried, incoming, start_index):
        piece_tiles = incoming.shape[1] // TILE
        blocks = incoming.reshape(groups_here, per_group, piece_tiles, TILE)

        def apply_piece(values):
            grad_sum, acc_now = values
            grad_term, acc_now = contribute(
                own_block, blocks, start_index // TILE - own_tile, table, acc_now
            )
            return (grad_sum + grad_term, acc_now)

        return lax.cond(
            start_index // TILE + piece_tiles > own_tile,
            apply_piece,
            lambda values: values,
            carried,
        )

    grads_zero = jnp.zeros(own_block.shape, jnp.float32)
    acc_zero = jnp.zeros((groups_here, total_tiles + 1, TILE, TILE), jnp.float32)
    incoming = lax.all_gather(output_grad, "ctx", axis=1, tiled=True)
    piece_width = incoming.shape[1]
    sub_width = min(piece_width, own_length)

    def sub_loop(k, values):
        sub_piece = lax.dynamic_slice_in_dim(incoming, k * sub_width, sub_width, 1)
        return add_piece(values, sub_piece, k * sub_width)

    grad_sum, lag_acc = lax.fori_loop(0, piece_width // sub_width, sub_loop, (grads_zero, acc_zero))
    input_grad = grad_sum.reshape(channels, own_length).astype(jnp.bfloat16)
    lag_part = lag_profile(lag_acc, total_tiles)
    owned_lags = lax.psum_scatter(lag_part, "ctx", scatter_dimension=1, tiled=True)
    everyone = lax.all_gather(owned_lags, "ch", axis=0, tiled=True)
    filter_grad = jnp.sum(everyone.reshape(G, -1, own_length), axis=1)
    return (input_grad, filter_grad)


def solution(mesh):
    in_specs = (P("ch", "ctx"), P("ch", "ctx"), P(None, "ctx"))
    out_specs = (P("ch", "ctx"), P(None, "ctx"))
    return jax.shard_map(
        per_device, mesh=mesh, in_specs=in_specs, out_specs=out_specs, check_vma=False
    )
```

profile of v0, /device:TPU:1, one launch (start us, length us, event | category | flops | bytes accessed | tf_op | source)
XLA Modules:
  0.0 516.6 jit_solution(17708326389877523336)
XLA Ops:
  8.1 29.3 %all_gather.10 = bf16[4,4096]{1,0:T(4,128)(2,1)S(1)} all-gather(bf16[4,512]{1,0:T(4,128)(2,1)S(1)} %constant_dynamic-slice_fusion.2), channel_id=1, replica_groups=mesh['ctx'=8,'ch'=32] {'ctx'}, dimensions={1}, use_global_device_ids=true | all-gather | bytes 36864 | tf_op jit(solution)/shard_map/all_gather | solution.py:75
  38.8 3.8 broadcast_in_dim.19
  42.6 13.6 %reshape.49 = bf16[4,32,32768]{2,1,0:T(8,128)(2,1)} reshape(bf16[4,32,128,256]{3,2,1,0:T(8,128)(2,1)} %broadcast_in_dim.19) | data formatting | bytes 16777216 | tf_op jit(solution)/shard_map/reshape | solution.py:20
  56.2 7.1 %slice.26 = bf16[4,32,32640]{2,1,0:T(8,128)(2,1)} slice(bf16[4,32,32768]{2,1,0:T(8,128)(2,1)} %reshape.49), slice={[0:4], [0:32], [0:32640]} | slice | bytes 16711680 | tf_op jit(solution)/shard_map/slice | solution.py:20
  63.3 29.5 %reshape.50 = bf16[4,32,128,255]{3,2,1,0:T(8,128)(2,1)} reshape(bf16[4,32,32640]{2,1,0:T(8,128)(2,1)} %slice.26) | data formatting | bytes 16711680 | tf_op jit(solution)/shard_map/reshape | solution.py:21
  92.8 4.9 slice.27
  97.7 2.3 copy.13
  100.1 4.4 broadcast_in_dim.18
  104.5 186.5 %while.39 = (s32[]{:T(128)}, f32[4,64,4,128]{3,1,2,0:T(8,128)S(1)}, f32[4,33,128,128]{2,3,0,1:T(8,128)}, s32[]{:T(128)}, bf16[256,4096]{1,0:T(8,128)(2,1)}, /*in...) while((s32[]{:T(128)}, f32[4,64,4,128]{3,1,2,0:T(8,128)S(1)}, ...), condition=%wide.region_5.6_spmd, body=%wide.region_0.5_spmd.sunk | while | flops 67436592 | bytes 7078900 | solution.py:108
  104.5 14.6 %conditional.2 = ((f32[4,64,4,128]{3,1,2,0:T(8,128)S(1)}, f32[4,33,128,128]{2,3,0,1:T(8,128)})) conditional(s32[]{:T(128)} %convert_element_type.27, (f32[4,64,4,128]{3,1,2,0:T(8,128)S(1)}, f32[4,33,128,128]{2,3,0,1:T(8,128)}) %tuple.92, (s32[]{:T(128)}, s32[]{:T(128)}, pred[]{:T(512)}, bf16[256,4096]{1,0:T(8,128)(2,1)}, ...), branch_computations={%region_1.1_spmd, %region_2.4_spmd} | conditional | flops 67436576 | bytes 7078499 | solution.py:91
  105.9 13.1 %while.38 = (s32[]{:T(128)}, f32[4,64,4,128]{3,1,2,0:T(8,128)S(1)}, f32[4,33,128,128]{2,3,0,1:T(8,128)}, bf16[4,64,10,128]{3,2,1,0:T(8,128)(2,1)S(1)}, s32[]{:T(...) while((s32[]{:T(128)}, f32[4,64,4,128]{3,1,2,0:T(8,128)S(1)}, ...), condition=%wide.region_4.3_spmd, body=%wide.region_3.2_spmd.sunk | while | flops 67305480 | bytes 3014918 | solution.py:61
  110.5 2.0 fusion.18
  113.8 1.9 fusion.18
  117.1 1.9 fusion.18
  119.2 24.5 %conditional.2 = ((f32[4,64,4,128]{3,1,2,0:T(8,128)S(1)}, f32[4,33,128,128]{2,3,0,1:T(8,128)})) conditional(s32[]{:T(128)} %convert_element_type.27, (f32[4,64,4,128]{3,1,2,0:T(8,128)S(1)}, f32[4,33,128,128]{2,3,0,1:T(8,128)}) %tuple.92, (s32[]{:T(128)}, s32[]{:T(128)}, pred[]{:T(512)}, bf16[256,4096]{1,0:T(8,128)(2,1)}, ...), branch_computations={%region_1.1_spmd, %region_2.4_spmd} | conditional | flops 67436576 | bytes 7078499 | solution.py:91
  120.6 22.9 %while.38 = (s32[]{:T(128)}, f32[4,64,4,128]{3,1,2,0:T(8,128)S(1)}, f32[4,33,128,128]{2,3,0,1:T(8,128)}, bf16[4,64,10,128]{3,2,1,0:T(8,128)(2,1)S(1)}, s32[]{:T(...) while((s32[]{:T(128)}, f32[4,64,4,128]{3,1,2,0:T(8,128)S(1)}, ...), condition=%wide.region_4.3_spmd, body=%wide.region_3.2_spmd.sunk | while | flops 67305480 | bytes 3014918 | solution.py:61
  122.0 2.0 fusion.18
  125.3 1.9 fusion.18
  131.8 2.0 fusion.18
  135.1 1.9 fusion.18
  141.6 1.9 fusion.18
  143.7 24.5 %conditional.2 = ((f32[4,64,4,128]{3,1,2,0:T(8,128)S(1)}, f32[4,33,128,128]{2,3,0,1:T(8,128)})) conditional(s32[]{:T(128)} %convert_element_type.27, (f32[4,64,4,128]{3,1,2,0:T(8,128)S(1)}, f32[4,33,128,128]{2,3,0,1:T(8,128)}) %tuple.92, (s32[]{:T(128)}, s32[]{:T(128)}, pred[]{:T(512)}, bf16[256,4096]{1,0:T(8,128)(2,1)}, ...), branch_computations={%region_1.1_spmd, %region_2.4_spmd} | conditional | flops 67436576 | bytes 7078499 | solution.py:91
  145.2 22.9 %while.38 = (s32[]{:T(128)}, f32[4,64,4,128]{3,1,2,0:T(8,128)S(1)}, f32[4,33,128,128]{2,3,0,1:T(8,128)}, bf16[4,64,10,128]{3,2,1,0:T(8,128)(2,1)S(1)}, s32[]{:T(...) while((s32[]{:T(128)}, f32[4,64,4,128]{3,1,2,0:T(8,128)S(1)}, ...), condition=%wide.region_4.3_spmd, body=%wide.region_3.2_spmd.sunk | while | flops 67305480 | bytes 3014918 | solution.py:61
  146.5 1.9 fusion.18
  153.1 2.0 fusion.18
  156.3 1.9 fusion.18
  166.1 2.0 fusion.18
  168.3 24.5 %conditional.2 = ((f32[4,64,4,128]{3,1,2,0:T(8,128)S(1)}, f32[4,33,128,128]{2,3,0,1:T(8,128)})) conditional(s32[]{:T(128)} %convert_element_type.27, (f32[4,64,4,128]{3,1,2,0:T(8,128)S(1)}, f32[4,33,128,128]{2,3,0,1:T(8,128)}) %tuple.92, (s32[]{:T(128)}, s32[]{:T(128)}, pred[]{:T(512)}, bf16[256,4096]{1,0:T(8,128)(2,1)}, ...), branch_computations={%region_1.1_spmd, %region_2.4_spmd} | conditional | flops 67436576 | bytes 7078499 | solution.py:91
  169.7 22.9 %while.38 = (s32[]{:T(128)}, f32[4,64,4,128]{3,1,2,0:T(8,128)S(1)}, f32[4,33,128,128]{2,3,0,1:T(8,128)}, bf16[4,64,10,128]{3,2,1,0:T(8,128)(2,1)S(1)}, s32[]{:T(...) while((s32[]{:T(128)}, f32[4,64,4,128]{3,1,2,0:T(8,128)S(1)}, ...), condition=%wide.region_4.3_spmd, body=%wide.region_3.2_spmd.sunk | while | flops 67305480 | bytes 3014918 | solution.py:61
  174.4 1.9 fusion.18
  177.6 2.0 fusion.18
  180.9 1.9 fusion.18
  184.2 1.9 fusion.18
  192.8 24.5 %conditional.2 = ((f32[4,64,4,128]{3,1,2,0:T(8,128)S(1)}, f32[4,33,128,128]{2,3,0,1:T(8,128)})) conditional(s32[]{:T(128)} %convert_element_type.27, (f32[4,64,4,128]{3,1,2,0:T(8,128)S(1)}, f32[4,33,128,128]{2,3,0,1:T(8,128)}) %tuple.92, (s32[]{:T(128)}, s32[]{:T(128)}, pred[]{:T(512)}, bf16[256,4096]{1,0:T(8,128)(2,1)}, ...), branch_computations={%region_1.1_spmd, %region_2.4_spmd} | conditional | flops 67436576 | bytes 7078499 | solution.py:91
  194.2 22.9 %while.38 = (s32[]{:T(128)}, f32[4,64,4,128]{3,1,2,0:T(8,128)S(1)}, f32[4,33,128,128]{2,3,0,1:T(8,128)}, bf16[4,64,10,128]{3,2,1,0:T(8,128)(2,1)S(1)}, s32[]{:T(...) while((s32[]{:T(128)}, f32[4,64,4,128]{3,1,2,0:T(8,128)S(1)}, ...), condition=%wide.region_4.3_spmd, body=%wide.region_3.2_spmd.sunk | while | flops 67305480 | bytes 3014918 | solution.py:61
  195.6 1.9 fusion.18
  208.7 2.0 fusion.18
  212.0 2.0 fusion.18
  217.4 24.5 %conditional.2 = ((f32[4,64,4,128]{3,1,2,0:T(8,128)S(1)}, f32[4,33,128,128]{2,3,0,1:T(8,128)})) conditional(s32[]{:T(128)} %convert_element_type.27, (f32[4,64,4,128]{3,1,2,0:T(8,128)S(1)}, f32[4,33,128,128]{2,3,0,1:T(8,128)}) %tuple.92, (s32[]{:T(128)}, s32[]{:T(128)}, pred[]{:T(512)}, bf16[256,4096]{1,0:T(8,128)(2,1)}, ...), branch_computations={%region_1.1_spmd, %region_2.4_spmd} | conditional | flops 67436576 | bytes 7078499 | solution.py:91
  218.8 23.0 %while.38 = (s32[]{:T(128)}, f32[4,64,4,128]{3,1,2,0:T(8,128)S(1)}, f32[4,33,128,128]{2,3,0,1:T(8,128)}, bf16[4,64,10,128]{3,2,1,0:T(8,128)(2,1)S(1)}, s32[]{:T(...) while((s32[]{:T(128)}, f32[4,64,4,128]{3,1,2,0:T(8,128)S(1)}, ...), condition=%wide.region_4.3_spmd, body=%wide.region_3.2_spmd.sunk | while | flops 67305480 | bytes 3014918 | solution.py:61
  220.2 2.0 fusion.18
  223.5 2.0 fusion.18
  230.0 2.0 fusion.18
  233.3 1.9 fusion.18
  241.9 24.5 %conditional.2 = ((f32[4,64,4,128]{3,1,2,0:T(8,128)S(1)}, f32[4,33,128,128]{2,3,0,1:T(8,128)})) conditional(s32[]{:T(128)} %convert_element_type.27, (f32[4,64,4,128]{3,1,2,0:T(8,128)S(1)}, f32[4,33,128,128]{2,3,0,1:T(8,128)}) %tuple.92, (s32[]{:T(128)}, s32[]{:T(128)}, pred[]{:T(512)}, bf16[256,4096]{1,0:T(8,128)(2,1)}, ...), branch_computations={%region_1.1_spmd, %region_2.4_spmd} | conditional | flops 67436576 | bytes 7078499 | solution.py:91
  243.4 22.9 %while.38 = (s32[]{:T(128)}, f32[4,64,4,128]{3,1,2,0:T(8,128)S(1)}, f32[4,33,128,128]{2,3,0,1:T(8,128)}, bf16[4,64,10,128]{3,2,1,0:T(8,128)(2,1)S(1)}, s32[]{:T(...) while((s32[]{:T(128)}, f32[4,64,4,128]{3,1,2,0:T(8,128)S(1)}, ...), condition=%wide.region_4.3_spmd, body=%wide.region_3.2_spmd.sunk | while | flops 67305480 | bytes 3014918 | solution.py:61
  244.7 1.9 fusion.18
  261.1 1.9 fusion.18
  264.3 2.0 fusion.18
  266.5 24.5 %conditional.2 = ((f32[4,64,4,128]{3,1,2,0:T(8,128)S(1)}, f32[4,33,128,128]{2,3,0,1:T(8,128)})) conditional(s32[]{:T(128)} %convert_element_type.27, (f32[4,64,4,128]{3,1,2,0:T(8,128)S(1)}, f32[4,33,128,128]{2,3,0,1:T(8,128)}) %tuple.92, (s32[]{:T(128)}, s32[]{:T(128)}, pred[]{:T(512)}, bf16[256,4096]{1,0:T(8,128)(2,1)}, ...), branch_computations={%region_1.1_spmd, %region_2.4_spmd} | conditional | flops 67436576 | bytes 7078499 | solution.py:91
  267.9 23.0 %while.38 = (s32[]{:T(128)}, f32[4,64,4,128]{3,1,2,0:T(8,128)S(1)}, f32[4,33,128,128]{2,3,0,1:T(8,128)}, bf16[4,64,10,128]{3,2,1,0:T(8,128)(2,1)S(1)}, s32[]{:T(...) while((s32[]{:T(128)}, f32[4,64,4,128]{3,1,2,0:T(8,128)S(1)}, ...), condition=%wide.region_4.3_spmd, body=%wide.region_3.2_spmd.sunk | while | flops 67305480 | bytes 3014918 | solution.py:61
  272.5 1.9 fusion.18
  275.8 2.0 fusion.18
  288.9 2.0 fusion.18
  291.0 9.1 %copy.16 = f32[4,33,128,128]{3,2,1,0:T(8,128)} copy(f32[4,33,128,128]{2,3,0,1:T(8,128)} %get-tuple-element.419) | data formatting | bytes 17301504 | tf_op jit(solution)/shard_map/while | solution.py:108
  300.2 11.4 %pad.19 = f32[132,128,256]{2,1,0:T(8,128)} pad(f32[132,128,128]{2,1,0:T(8,128)} %bitcast.42, f32[]{:T(128)} %constant.217.clone.1), padding=0_0x0_0x128_0 | pad | bytes 25952260 | tf_op jit(solution)/shard_map/jit(_pad)/pad | solution.py:29
  311.6 7.3 %pad.23 = f32[136,128,256]{2,1,0:T(8,128)S(1)} pad(f32[132,128,256]{2,1,0:T(8,128)} %pad.19, f32[]{:T(128)} %constant.217.clone.1), padding=0_4x0_0x0_0 | pad | bytes 35127300
  318.9 22.0 %copy.24 = f32[17,8,128,256]{3,1,2,0:T(8,128)S(1)} copy(f32[17,8,128,256]{3,2,1,0:T(8,128)S(1)} %bitcast.41) | data formatting | bytes 35651584
  340.9 6.4 %pad.20 = f32[132,32896]{1,0:T(8,128)} pad(f32[132,32768]{1,0:T(8,128)S(1)} %bitcast.40, f32[]{:T(128)} %constant.217.clone.1), padding=0_0x0_128 | pad | bytes 34670596 | tf_op jit(solution)/shard_map/jit(_pad)/pad | solution.py:30
  347.3 27.8 %reshape.54 = f32[132,128,257]{2,1,0:T(8,128)} reshape(f32[132,32896]{1,0:T(8,128)} %pad.20) | data formatting | bytes 34738176 | tf_op jit(solution)/shard_map/reshape | solution.py:31
  375.1 9.4 %reduce_sum.8 = f32[132,257]{1,0:T(8,128)S(1)} reduce(f32[132,128,257]{2,1,0:T(8,128)} %reshape.54, f32[]{:T(128)} %constant.217.clone.1), dimensions={1}, to_apply=%region_6.7 | reduce | flops 4308348 | bytes 17504788 | tf_op jit(solution)/shard_map/reduce_sum | solution.py:32
  384.5 2.0 copy.21
  387.6 84.1 %reduce-scatter.4.cloned.1.call-done = f32[512,4]{1,0:T(8,128)} async-done(((f32[4096,4]{1,0:T(8,128)}), f32[512,4]{1,0:T(8,128)}) %reduce-scatter.4.cloned.1.call-update) | async-done | bytes 8208
  472.7 36.3 %all-gather = f32[32,4,512]{2,1,0:T(4,128)S(1)} all-gather(f32[1,4,512]{2,1,0:T(4,128)S(1)} %bitcast.47), channel_id=1, replica_groups=mesh['ctx'=8,'ch'=32] {'ch'}, dimensions={0}, use_global_device_ids=true | all-gather | bytes 270336 | tf_op jit(solution)/shard_map/all_gather | solution.py:112
  (195 shorter events, 133.3 us)
Async XLA Ops:
  7.2 0.9 copy-start
  7.2 92.8 %all-gather.3.cloned.1.call-start = ((), (), s32[]{:S(2)}) async-start(), calls=%async_computation.1 | async-start | bytes 2359296 | tf_op jit(solution)/shard_map/all_gather | solution.py:100
  7.9 463.7 %reduce-scatter.4.cloned.1.call-start = ((), (), s32[]{:S(2)}) async-start(), calls=%async_computation.2 | async-start | bytes 2359296
  375.1 134.8 %copy-start.1 = (bf16[128,512]{1,0:T(8,128)(2,1)S(1)}, bf16[128,512]{1,0:T(8,128)(2,1)}, u32[]{:S(2)}) copy-start(bf16[128,512]{1,0:T(8,128)(2,1)} %param.11) | copy-start | bytes 393220
Sparse Core Ops, SparseCore 0:
  10.5 64.2 all-gather.2
  386.7 84.9 reduce-scatter.3
where the time goes:
time: 521 us; the launch traced here: 517 us
  local copies, waits for them, and re-layouts  176 us (34%)
  matrix products  163 us (31%)
  waiting for transfers between devices  84.8 us (16%)
  blocking collectives  65.6 us (13%)
  between operations  14.2 us (3%)
  other arithmetic  10.5 us (2%)
    dot_general x53, matrix products, one_turn(): jnp.einsum('gcau,gcav->guv', own_block, window, preferred_element_type=jn...  103 us
    unnamed x3, waiting for transfers between devices  84.8 us
    dot_general x53, matrix products, one_turn(): jnp.einsum('gcav,gvu->gcau', window, tiles, preferred_element_type=jnp.fl...  60.2 us
    all_gather x1, blocking collectives, per_device(): everyone = lax.all_gather(owned_lags, 'ch', axis=0, tiled=True)  36.3 us
    unnamed x10, local copies, waits for them, and re-layouts  34 us
    reshape x1, local copies, waits for them, and re-layouts, toeplitz_table(): slanted = flat.reshape(groups, total_tiles, TILE, 2 * TILE - 1)  29.5 us
    all_gather x1, blocking collectives, per_device(): filter_lags = lax.all_gather(filter_part, 'ctx', axis=1, tiled=True)  29.3 us
    reshape x1, local copies, waits for them, and re-layouts, lag_profile(): slanted = widened.reshape(groups * slots, TILE, 2 * TILE + 1)  27.8 us
  transfers between devices with their start and end apart: 2, of which 1 were waited for; matrix products, arithmetic and copies ran while one was open for 12% of the time, Pallas kernels for 0%

commit v1 on v0

v1 whole, which is shorter than its diff:
```python
import jax
import jax.numpy as jnp
from jax import lax
from jax.experimental import pallas as pl
from jax.experimental.pallas import tpu as pltpu
from jax.sharding import PartitionSpec as P

C = 8192
G = 128
TILE = 256


def roll_left(x, amount):
    lanes = x.shape[1]
    return x if amount == 0 else pltpu.roll(x, lanes - amount, 1)


def gradients_kernel(recv_ref, out_ref, og_ref, cit_ref, table_ref, skew_ref, acc_ref):
    blocks, _, own = recv_ref.shape
    per = 32
    tokens = blocks * own
    tiles = tokens // TILE
    rows = tiles * per

    ci = []
    for a in range(tiles):
        j, lo = (a * TILE) // own, (a * TILE) % own
        og_ref[a * per : (a + 1) * per, :] = recv_ref[j, per : 2 * per, lo : lo + TILE]
        ci.append(recv_ref[j, 0:per, lo : lo + TILE])
    og_ref[rows : 2 * rows, :] = jnp.zeros((rows, TILE), og_ref.dtype)
    cit_ref[...] = jnp.concatenate(ci, axis=0).T

    taps = jnp.concatenate(
        [recv_ref[j, 2 * per : 2 * per + 1, :].astype(jnp.float32) for j in range(blocks)], axis=1
    )
    wide = jnp.broadcast_to(taps, (8, tokens))
    base = pltpu.roll(wide, 0, 1, stride=1, stride_axis=0)
    for t in range(0, 16, 2):
        pair = jnp.concatenate(
            [base if t == 0 else pltpu.roll(base, 8 * t, 1), pltpu.roll(base, 8 * t + 8, 1)], axis=0
        )
        u = 8 * t + lax.broadcasted_iota(jnp.int32, (16, 128), 0)
        first = jnp.where(lax.broadcasted_iota(jnp.int32, (16, 128), 1) >= u, pair[:, 0:128], 0.0)
        pair = jnp.concatenate([first, pair[:, 128:]], axis=1).astype(jnp.bfloat16)
        table_ref[8 * t : 8 * t + 16, :] = pair
        table_ref[128 + 8 * t : 128 + 8 * t + 16, 128:] = pair[:, : tokens - 128]
        table_ref[128 + 8 * t : 128 + 8 * t + 16, 0:128] = jnp.zeros((16, 128), jnp.bfloat16)

    for d in range(tiles):
        depth = rows if d < tiles // 2 else rows // 2
        cross = jnp.dot(
            cit_ref[:, 0:depth],
            og_ref[d * per : d * per + depth, :],
            preferred_element_type=jnp.float32,
        )
        if d == 0:
            u = lax.broadcasted_iota(jnp.int32, (TILE, TILE), 0)
            v = lax.broadcasted_iota(jnp.int32, (TILE, TILE), 1)
            cross = jnp.where(v >= u, cross, 0.0)
        upper, lower = cross[0:128, :], cross[128:256, :]
        at = d * TILE
        skew_ref[:, at : at + 128] = upper[:, 0:128] + lower[:, 128:256]
        skew_ref[:, at + 128 : at + 256] = upper[:, 128:256]
        if d > 0:
            skew_ref[:, at - 128 : at] = skew_ref[:, at - 128 : at] + lower[:, 0:128]
    folded = skew_ref[0:8, :]
    for t in range(1, 16):
        folded = folded + roll_left(skew_ref[8 * t : 8 * t + 8, :], 8 * t)
    lags = folded[0:1, :]
    for r in range(1, 8):
        lags = lags + roll_left(folded[r : r + 1, :], r)
    high = lags.astype(jnp.bfloat16).astype(jnp.float32)
    low = lags - high
    row = lax.broadcasted_iota(jnp.int32, (8, own), 0)
    for j in range(blocks):
        part = slice(j * own, (j + 1) * own)
        packed = jnp.where(row == 0, high[:, part], jnp.where(row == 1, low[:, part], 0.0))
        out_ref[j, per : per + 8, :] = packed.astype(jnp.bfloat16)

    for d in range(tiles):
        live = rows - d * per
        term = lax.dot_general(
            og_ref[d * per : rows, :],
            table_ref[:, d * TILE : (d + 1) * TILE],
            (((1,), (1,)), ((), ())),
            preferred_element_type=jnp.float32,
        )
        if d == 0:
            acc_ref[...] = term
        else:
            acc_ref[0:live, :] = acc_ref[0:live, :] + term
    for a in range(tiles):
        j, lo = (a * TILE) // own, (a * TILE) % own
        out_ref[j, 0:per, lo : lo + TILE] = acc_ref[a * per : (a + 1) * per, :].astype(jnp.bfloat16)


def gradients(recv):
    blocks, _, own = recv.shape
    tokens = blocks * own
    rows = tokens // TILE * 32
    return pl.pallas_call(
        gradients_kernel,
        out_shape=jax.ShapeDtypeStruct((blocks, 40, own), jnp.bfloat16),
        in_specs=[pl.BlockSpec(memory_space=pltpu.VMEM)],
        out_specs=pl.BlockSpec(memory_space=pltpu.VMEM),
        scratch_shapes=[
            pltpu.VMEM((2 * rows, TILE), jnp.bfloat16),
            pltpu.VMEM((TILE, rows), jnp.bfloat16),
            pltpu.VMEM((TILE, tokens), jnp.bfloat16),
            pltpu.VMEM((128, tokens), jnp.float32),
            pltpu.VMEM((rows, TILE), jnp.float32),
        ],
        name="gradients",
    )(recv)


def per_device(conv_input, output_grad, long_filter):
    channels, own = conv_input.shape
    cycle = lax.axis_size("ctx")
    share = channels // cycle
    groups_here = channels // (C // G)
    first_group = lax.axis_index("ch") * groups_here
    taps = lax.dynamic_slice_in_dim(long_filter, first_group, groups_here, 0)
    taps = jnp.repeat(taps, cycle // groups_here, axis=0)[:, None, :]
    send = jnp.concatenate(
        [
            conv_input.reshape(cycle, share, own),
            output_grad.reshape(cycle, share, own),
            taps,
        ],
        axis=1,
    )
    recv = lax.all_to_all(send, "ctx", 0, 0, tiled=True)
    back = lax.all_to_all(gradients(recv), "ctx", 0, 0, tiled=True)
    input_grad = back[:, :share, :].reshape(channels, own)
    parts = back[:, share : share + 2, :].astype(jnp.float32)
    owned = jnp.sum(parts.reshape(groups_here, -1, own), axis=1)
    peers = lax.axis_size("ch")
    everyone = lax.all_to_all(
        jnp.broadcast_to(owned[None], (peers, groups_here, own)), "ch", 0, 0, tiled=True
    )
    return input_grad, everyone.reshape(G, own)


def solution(mesh):
    in_specs = (P("ch", "ctx"), P("ch", "ctx"), P(None, "ctx"))
    out_specs = (P("ch", "ctx"), P(None, "ctx"))
    return jax.shard_map(
        per_device, mesh=mesh, in_specs=in_specs, out_specs=out_specs, check_vma=False
    )
```

time: 521 us -> 61.8 us (0.12)
  local copies, waits for them, and re-layouts: 176 us -> 3.2 us
  matrix products: 163 us -> 0 us
  waiting for transfers between devices: 84.8 us -> 10.8 us
  blocking collectives: 65.6 us -> 30.1 us
  between operations: 14.2 us -> 0.67 us
  starting transfers between devices: 0.08 us -> 12 us
  other arithmetic: 10.5 us -> 1.16 us
    dot_general x106 -> x0, matrix products: 163 us -> none  [the longest x53 103 us: one_turn(): jnp.einsum('gcau,gcav->guv', own_block, window, preferred_element_type=jn...]
    unnamed x3 -> x0, waiting for transfers between devices: 84.8 us -> none
    reshape x14 -> x1, local copies, waits for them, and re-layouts: 72.4 us -> 0.79 us  [per_device(): return (input_grad, everyone.reshape(G, own))]
    all_gather x2 -> x0, blocking collectives: 65.6 us -> none  [the longest x1 36.3 us: per_device(): everyone = lax.all_gather(owned_lags, 'ch', axis=0, tiled=True)]
    unnamed x10 -> x2, local copies, waits for them, and re-layouts: 34 us -> 0.9 us
    all_to_all x0 -> x2, blocking collectives: none -> 30.1 us  [the longest x1 18.6 us: per_device(): recv = lax.all_to_all(send, 'ctx', 0, 0, tiled=True)]
    pad x11 -> x0, local copies, waits for them, and re-layouts: 20.1 us -> none  [the longest x1 11.4 us: lag_profile(): jnp.pad(flat, ((0, 0), (0, 0), (TILE, 0)))]
    dynamic_slice x62 -> x1, local copies, waits for them, and re-layouts: 17.3 us -> 0.01 us  [per_device(): taps = lax.dynamic_slice_in_dim(long_filter, first_group, groups_here, 0)]
  transfers between devices with their start and end apart: 2 -> 1, of which waited for: 1 -> 1; matrix products, arithmetic and copies ran while one was open for 12% -> 1% of each run, Pallas kernels for 0% -> 0%
where the time goes in v1:
time: 61.8 us; the launch traced here: 61.5 us
  blocking collectives  30.1 us (49%)
  starting transfers between devices  12 us (19%)
  waiting for transfers between devices  10.8 us (17%)
  Pallas kernels  3.53 us (6%)
  local copies, waits for them, and re-layouts  3.2 us (5%)
  other arithmetic  1.16 us (2%)
  between operations  0.67 us (1%)
    all_to_all x1, blocking collectives, per_device(): recv = lax.all_to_all(send, 'ctx', 0, 0, tiled=True)  18.6 us
    all_to_all x1, starting transfers between devices, per_device(): lax.all_to_all(jnp.broadcast_to(owned[None], (peers, groups_here, own)),...  12 us
    all_to_all x1, blocking collectives, per_device(): back = lax.all_to_all(gradients(recv), 'ctx', 0, 0, tiled=True)  11.5 us
    all_to_all x1, waiting for transfers between devices, per_device(): lax.all_to_all(jnp.broadcast_to(owned[None], (peers, groups_here, own)),...  10.8 us
    pallas_call x1, Pallas kernels, gradients(): pl.pallas_call(gradients_kernel, out_shape=jax.ShapeDtypeStruct((blocks,...  3.53 us
  transfers between devices with their start and end apart: 1, of which 1 were waited for; matrix products, arithmetic and copies ran while one was open for 1% of the time, Pallas kernels for 0%

profile of v1, /device:TPU:1, one launch (start us, length us, event | category | flops | bytes accessed | tf_op | source)
XLA Modules:
  0.0 61.5 jit_solution(4217533274557202843)
XLA Ops:
  0.6 0.0 copy-start
  0.6 0.9 %copy-done = bf16[128,512]{1,0:T(8,128)(2,1)S(1)} copy-done((bf16[128,512]{1,0:T(8,128)(2,1)S(1)}, bf16[128,512]{1,0:T(8,128)(2,1)}, u32[]{:S(2)}) %copy-start) | copy-done | bytes 131096
  1.6 1.1 %pad_maximum_fusion = bf16[8,65,512]{2,1,0:T(8,128)(2,1)S(1)} fusion(bf16[8,1,512]{2,1,0:T(2,128)(2,1)S(1)} %broadcast_in_dim_reshape.4, bf16[8,32,512]{2,1,0:T(8,128)(2,1)} %bitcast.3, bf16[8,32,512]{2,1,0:T(8,128)(2,1)} %bitcast.4), kind=kLoop, calls=%fused_computation | loop fusion | flops 1597440 | bytes 1064960 | tf_op jit(solution)/shard_map/concatenate | solution.py:125
  2.7 18.6 %all_to_all.15.recv_ref = bf16[8,65,512]{2,1,0:T(8,128)(2,1)} all-to-all(bf16[8,65,512]{2,1,0:T(8,128)(2,1)S(1)} %pad_maximum_fusion), channel_id=1, replica_groups=mesh['ctx'=8,'ch'=32] {'ctx'}, dimensions={0} | all-to-all | bytes 1064960 | tf_op jit(solution)/shard_map/all_to_all | solution.py:133
  21.2 3.5 %gradients.1 = bf16[8,40,512]{2,1,0:T(8,128)(2,1)} custom-call(bf16[8,65,512]{2,1,0:T(8,128)(2,1)} %all_to_all.15.recv_ref), custom_call_target="tpu_custom_call" | custom-call | tf_op jit(solution)/shard_map/gradients/pallas_call | solution.py:101
  24.8 11.5 %all_to_all.16 = bf16[8,40,512]{2,1,0:T(8,128)(2,1)S(1)} all-to-all(bf16[8,40,512]{2,1,0:T(8,128)(2,1)} %gradients.1), channel_id=1, replica_groups=mesh['ctx'=8,'ch'=32] {'ctx'}, dimensions={0} | all-to-all | bytes 655360 | tf_op jit(solution)/shard_map/all_to_all | solution.py:134
  36.4 0.7 %broadcast_in_dim.10 = f32[32,4,512]{2,1,0:T(4,128)} broadcast(f32[4,512]{1,0:T(4,128)S(1)} %reduce_sum.18), dimensions={1,2} | broadcast | bytes 270336 | tf_op jit(solution)/shard_map/broadcast_in_dim | solution.py:140
  37.1 12.0 %all-to-all-start.2 = ((f32[32,4,512]{2,1,0:T(4,128)}), f32[32,4,512]{2,1,0:T(4,128)S(1)}, u32[]{:S(2)}, u32[]{:S(2)}) async-start(f32[32,4,512]{2,1,0:T(4,128)} %broadcast_in_dim.10), calls=%async_computation.2 | async-start | bytes 524288 | tf_op jit(solution)/shard_map/all_to_all | solution.py:139
  49.1 0.7 %slice.8 = bf16[8,32,512]{2,1,0:T(8,128)(2,1)} slice(bf16[8,40,512]{2,1,0:T(8,128)(2,1)S(1)} %all_to_all.16), slice={[0:8], [0:32], [0:512]} | slice | bytes 524288 | tf_op jit(solution)/shard_map/slice | solution.py:135
  49.8 10.8 %all-to-all-done.2 = f32[32,4,512]{2,1,0:T(4,128)S(1)} async-done(((f32[32,4,512]{2,1,0:T(4,128)}), f32[32,4,512]{2,1,0:T(4,128)S(1)}, u32[]{:S(2)}, u32[]{:S(2)}) %all-to-all-start.2) | async-done | bytes 262176 | tf_op jit(solution)/shard_map/all_to_all | solution.py:139
  60.7 0.8 %reshape.22 = f32[128,512]{1,0:T(8,128)} reshape(f32[32,4,512]{2,1,0:T(4,128)S(1)} %all-to-all-done.2) | data formatting | bytes 524288 | tf_op jit(solution)/shard_map/reshape | solution.py:142
  (6 shorter events, 0.1 us)
Async XLA Ops:
  0.6 0.9 %copy-start = (bf16[128,512]{1,0:T(8,128)(2,1)S(1)}, bf16[128,512]{1,0:T(8,128)(2,1)}, u32[]{:S(2)}) copy-start(bf16[128,512]{1,0:T(8,128)(2,1)} %param.5) | copy-start | bytes 393220
  37.1 23.5 %all-to-all-start.2 = ((f32[32,4,512]{2,1,0:T(4,128)}), f32[32,4,512]{2,1,0:T(4,128)S(1)}, u32[]{:S(2)}, u32[]{:S(2)}) async-start(f32[32,4,512]{2,1,0:T(4,128)} %broadcast_in_dim.10), calls=%async_computation.2 | async-start | bytes 524288 | tf_op jit(solution)/shard_map/all_to_all | solution.py:139

commit v2 on v1

--- a/solution.py
+++ b/solution.py
@@ -8,6 +8,44 @@
 C = 8192
 G = 128
 TILE = 256
+
+
+def pack_kernel(ci_ref, og_ref, filter_ref, send_ref, taps_ref, sems):
+    blocks, per, _ = ci_ref.shape
+    k = lax.axis_index("ch")
+    at = pl.multiple_of(8 * lax.div(k, 2), 8)
+    copies = [
+        pltpu.make_async_copy(filter_ref.at[pl.ds(at, 8), :], taps_ref, sems.at[0]),
+        pltpu.make_async_copy(ci_ref, send_ref.at[:, 0:per, :], sems.at[1]),
+        pltpu.make_async_copy(og_ref, send_ref.at[:, per : 2 * per, :], sems.at[2]),
+    ]
+    for copy in copies:
+        copy.start()
+    copies[0].wait()
+    taps = taps_ref[...].astype(jnp.float32)
+    taps = jnp.where(lax.rem(k, 2) == 0, taps[0:4, :], taps[4:8, :]).astype(jnp.bfloat16)
+    for i in range(blocks):
+        row = i * 4 // blocks
+        send_ref[i, 2 * per : 2 * per + 1, :] = taps[row : row + 1, :]
+    copies[1].wait()
+    copies[2].wait()
+
+
+def pack(conv_input, output_grad, long_filter, blocks):
+    channels, own = conv_input.shape
+    share = channels // blocks
+    return pl.pallas_call(
+        pack_kernel,
+        out_shape=pltpu.VMEM((blocks, 2 * share + 1, own), jnp.bfloat16),
+        in_specs=[pl.BlockSpec(memory_space=pl.ANY)] * 3,
+        out_specs=pl.BlockSpec(memory_space=pltpu.VMEM),
+        scratch_shapes=[pltpu.VMEM((8, own), jnp.bfloat16), pltpu.SemaphoreType.DMA((3,))],
+        name="pack",
+    )(
+        conv_input.reshape(blocks, share, own),
+        output_grad.reshape(blocks, share, own),
+        long_filter,
+    )
 
 
 def roll_left(x, amount):
@@ -66,9 +104,10 @@
     folded = skew_ref[0:8, :]
     for t in range(1, 16):
         folded = folded + roll_left(skew_ref[8 * t : 8 * t + 8, :], 8 * t)
-    lags = folded[0:1, :]
-    for r in range(1, 8):
-        lags = lags + roll_left(folded[r : r + 1, :], r)
+    r = lax.broadcasted_iota(jnp.int32, folded.shape, 0)
+    for bit in (1, 2, 4):
+        folded = jnp.where((r & bit) > 0, roll_left(folded, bit), folded)
+    lags = jnp.sum(folded, axis=0, keepdims=True)
     high = lags.astype(jnp.bfloat16).astype(jnp.float32)
     low = lags - high
     row = lax.broadcasted_iota(jnp.int32, (8, own), 0)
@@ -100,7 +139,7 @@
     rows = tokens // TILE * 32
     return pl.pallas_call(
         gradients_kernel,
-        out_shape=jax.ShapeDtypeStruct((blocks, 40, own), jnp.bfloat16),
+        out_shape=pltpu.VMEM((blocks, 40, own), jnp.bfloat16),
         in_specs=[pl.BlockSpec(memory_space=pltpu.VMEM)],
         out_specs=pl.BlockSpec(memory_space=pltpu.VMEM),
         scratch_shapes=[
@@ -111,7 +150,7 @@
             pltpu.VMEM((rows, TILE), jnp.float32),
         ],
         name="gradients",
-    )(recv)
+    )(pltpu.with_memory_space_constraint(recv, pltpu.VMEM))
 
 
 def per_device(conv_input, output_grad, long_filter):
@@ -119,27 +158,29 @@
     cycle = lax.axis_size("ctx")
     share = channels // cycle
     groups_here = channels // (C // G)
-    first_group = lax.axis_index("ch") * groups_here
-    taps = lax.dynamic_slice_in_dim(long_filter, first_group, groups_here, 0)
-    taps = jnp.repeat(taps, cycle // groups_here, axis=0)[:, None, :]
-    send = jnp.concatenate(
-        [
-            conv_input.reshape(cycle, share, own),
-            output_grad.reshape(cycle, share, own),
-            taps,
-        ],
-        axis=1,
-    )
+    send = pack(conv_input, output_grad, long_filter, cycle)
     recv = lax.all_to_all(send, "ctx", 0, 0, tiled=True)
     back = lax.all_to_all(gradients(recv), "ctx", 0, 0, tiled=True)
     input_grad = back[:, :share, :].reshape(channels, own)
     parts = back[:, share : share + 2, :].astype(jnp.float32)
     owned = jnp.sum(parts.reshape(groups_here, -1, own), axis=1)
     peers = lax.axis_size("ch")
-    everyone = lax.all_to_all(
-        jnp.broadcast_to(owned[None], (peers, groups_here, own)), "ch", 0, 0, tiled=True
+    groups = [list(range(core, peers, 2)) for core in range(2)]
+    mine = lax.all_to_all(
+        jnp.broadcast_to(owned[None], (peers // 2, groups_here, own)),
+        "ch",
+        0,
+        0,
+        axis_index_groups=groups,
+        tiled=True,
     )
-    return input_grad, everyone.reshape(G, own)
+    theirs = lax.ppermute(mine, "ch", [(k, k ^ 1) for k in range(peers)])
+    filter_grad = jnp.where(
+        lax.axis_index("ch") % 2 == 0,
+        jnp.concatenate([mine, theirs], axis=1),
+        jnp.concatenate([theirs, mine], axis=1),
+    )
+    return input_grad, filter_grad.reshape(G, own)
 
 
 def solution(mesh):

time: 61.8 us -> 55 us (0.89)
  blocking collectives: 30.1 us -> 44.8 us
  waiting for transfers between devices: 10.8 us -> 0.26 us
  starting transfers between devices: 12 us -> 4.58 us
  local copies, waits for them, and re-layouts: 3.2 us -> 0.76 us
  Pallas kernels: 3.53 us -> 2.83 us
    all_to_all x0 -> x1, blocking collectives: none -> 15.6 us  [per_device(): lax.all_to_all(jnp.broadcast_to(owned[None], (peers // 2, groups_here, ow...]
    all_to_all x1 -> x0, starting transfers between devices: 12 us -> none  [per_device(): lax.all_to_all(jnp.broadcast_to(owned[None], (peers, groups_here, own)),...]
    all_to_all x1 -> x0, waiting for transfers between devices: 10.8 us -> none  [per_device(): lax.all_to_all(jnp.broadcast_to(owned[None], (peers, groups_here, own)),...]
    ppermute x0 -> x1, starting transfers between devices: none -> 4.58 us  [per_device(): theirs = lax.ppermute(mine, 'ch', [(k, k ^ 1) for k in range(peers)])]
    concatenate x1 -> x0, other arithmetic: 1.08 us -> none  [per_device(): jnp.concatenate([conv_input.reshape(cycle, share, own), output_grad.resha...]
    unnamed x2 -> x0, local copies, waits for them, and re-layouts: 0.9 us -> none
    select_n x0 -> x1, other arithmetic: none -> 0.8 us  [per_device(): jnp.where(lax.axis_index('ch') % 2 == 0, jnp.concatenate([mine, theirs],...]
    reshape x1 -> x0, local copies, waits for them, and re-layouts: 0.79 us -> none  [per_device(): return (input_grad, everyone.reshape(G, own))]
where the time goes in v2:
time: 55 us; the launch traced here: 54.8 us
  blocking collectives  44.8 us (81%)
  starting transfers between devices  4.58 us (8%)
  Pallas kernels  2.83 us (5%)
  other arithmetic  0.87 us (2%)
  local copies, waits for them, and re-layouts  0.76 us (1%)
  between operations  0.67 us (1%)
    all_to_all x1, blocking collectives, per_device(): recv = lax.all_to_all(send, 'ctx', 0, 0, tiled=True)  18.5 us
    all_to_all x1, blocking collectives, per_device(): lax.all_to_all(jnp.broadcast_to(owned[None], (peers // 2, groups_here, ow...  15.6 us
    all_to_all x1, blocking collectives, per_device(): back = lax.all_to_all(gradients(recv), 'ctx', 0, 0, tiled=True)  10.7 us
    ppermute x1, starting transfers between devices, per_device(): theirs = lax.ppermute(mine, 'ch', [(k, k ^ 1) for k in range(peers)])  4.58 us
    pallas_call x1, Pallas kernels, gradients(): pl.pallas_call(gradients_kernel, out_shape=pltpu.VMEM((blocks, 40, own),...  1.75 us
  transfers between devices with their start and end apart: 1, of which 1 were waited for; matrix products, arithmetic and copies ran while one was open for 1% of the time, Pallas kernels for 0%

profile of v2, /device:TPU:1, one launch (start us, length us, event | category | flops | bytes accessed | tf_op | source)
XLA Modules:
  0.0 54.8 jit_solution(14068855528566590746)
XLA Ops:
  0.6 1.1 %pack.1 = bf16[8,65,512]{2,1,0:T(8,128)(2,1)S(1)} custom-call(bf16[8,32,512]{2,1,0:T(8,128)(2,1)} %bitcast.5, bf16[8,32,512]{2,1,0:T(8,128)(2,1)} %bitcast.6, bf16[128,512]{1,0:T(8,128)(2,1)} %filter_ref.1), custom_call_target="tpu_custom_call" | custom-call | tf_op jit(solution)/shard_map/pack/pallas_call | solution.py:37
  1.7 18.5 %all_to_all.15.recv_ref = bf16[8,65,512]{2,1,0:T(8,128)(2,1)S(1)} all-to-all(bf16[8,65,512]{2,1,0:T(8,128)(2,1)S(1)} %pack.1), channel_id=1, replica_groups=mesh['ctx'=8,'ch'=32] {'ctx'}, dimensions={0} | all-to-all | bytes 1064960 | tf_op jit(solution)/shard_map/all_to_all | solution.py:162
  20.2 1.7 %gradients.1 = bf16[8,40,512]{2,1,0:T(8,128)(2,1)S(1)} custom-call(bf16[8,65,512]{2,1,0:T(8,128)(2,1)S(1)} %all_to_all.15.recv_ref), custom_call_target="tpu_custom_call" | custom-call | tf_op jit(solution)/shard_map/gradients/pallas_call | solution.py:140
  21.9 10.7 %all_to_all.16 = bf16[8,40,512]{2,1,0:T(8,128)(2,1)S(1)} all-to-all(bf16[8,40,512]{2,1,0:T(8,128)(2,1)S(1)} %gradients.1), channel_id=1, replica_groups=mesh['ctx'=8,'ch'=32] {'ctx'}, dimensions={0} | all-to-all | bytes 655360 | tf_op jit(solution)/shard_map/all_to_all | solution.py:163
  32.8 15.6 %all_to_all.17 = f32[16,4,512]{2,1,0:T(4,128)S(1)} all-to-all(f32[16,4,512]{2,1,0:T(4,128)S(1)} %broadcast_in_dim.2), channel_id=1, replica_groups={{0,2,4,6,8,10,12,14,16,18,20,22,24,26,28,30},{1,3,5,7,9,11,13,15,17,19,..., dimensions={0} | all-to-all | bytes 262144 | tf_op jit(solution)/shard_map/all_to_all | solution.py:169
  48.4 4.6 %collective-permute-start = (f32[16,4,512]{2,1,0:T(4,128)S(1)}, f32[16,4,512]{2,1,0:T(4,128)S(1)}, u32[]{:S(2)}, u32[]{:S(2)}) collective-permute-start(f32[16,4,512]{2,1,0:T(4,128)S(1)} %all_to_all.17), channel_id=1, source_target_pairs={{0,1},{1,0},{2,3},{3,2},{4,5},{5,4},{6,7},{7,6},{8,9},{9,8},{10,11... | collective-permute-start | bytes 393224 | tf_op jit(solution)/shard_map/ppermute | solution.py:177
  53.0 0.7 %slice.8 = bf16[8,32,512]{2,1,0:T(8,128)(2,1)} slice(bf16[8,40,512]{2,1,0:T(8,128)(2,1)S(1)} %all_to_all.16), slice={[0:8], [0:32], [0:512]} | slice | bytes 524288 | tf_op jit(solution)/shard_map/slice | solution.py:164
  53.7 0.3 collective-permute-done
  54.0 0.8 %fusion = f32[128,512]{1,0:T(8,128)} fusion(f32[16,4,512]{2,1,0:T(4,128)S(1)} %collective-permute-done, f32[16,4,512]{2,1,0:T(4,128)S(1)} %all_to_all.17, pred[]{:T(512)S(6)} %eq.5), kind=kLoop, calls=%fused_computation.1 | loop fusion | flops 196608 | bytes 524289 | tf_op jit(solution)/shard_map/jit(_where)/select_n | solution.py:178
  (4 shorter events, 0.1 us)
Async XLA Ops:
  48.4 5.6 %collective-permute-start = (f32[16,4,512]{2,1,0:T(4,128)S(1)}, f32[16,4,512]{2,1,0:T(4,128)S(1)}, u32[]{:S(2)}, u32[]{:S(2)}) collective-permute-start(f32[16,4,512]{2,1,0:T(4,128)S(1)} %all_to_all.17), channel_id=1, source_target_pairs={{0,1},{1,0},{2,3},{3,2},{4,5},{5,4},{6,7},{7,6},{8,9},{9,8},{10,11... | collective-permute-start | bytes 393224 | tf_op jit(solution)/shard_map/ppermute | solution.py:177

commit v3 on v2

--- a/solution.py
+++ b/solution.py
@@ -11,35 +11,48 @@
 
 
 def pack_kernel(ci_ref, og_ref, filter_ref, send_ref, taps_ref, sems):
-    blocks, per, _ = ci_ref.shape
+    blocks, per, own = ci_ref.shape
+    pieces = own // 128
+    span = pieces * per
     k = lax.axis_index("ch")
     at = pl.multiple_of(8 * lax.div(k, 2), 8)
-    copies = [
-        pltpu.make_async_copy(filter_ref.at[pl.ds(at, 8), :], taps_ref, sems.at[0]),
-        pltpu.make_async_copy(ci_ref, send_ref.at[:, 0:per, :], sems.at[1]),
-        pltpu.make_async_copy(og_ref, send_ref.at[:, per : 2 * per, :], sems.at[2]),
-    ]
+    taps_copy = pltpu.make_async_copy(filter_ref.at[pl.ds(at, 8), :], taps_ref, sems.at[0])
+    taps_copy.start()
+    copies = []
+    for n, ref in enumerate((ci_ref, og_ref)):
+        for q in range(pieces):
+            copy = pltpu.make_async_copy(
+                ref.at[:, :, q * 128 : (q + 1) * 128],
+                send_ref.at[:, n * span + q * per : n * span + (q + 1) * per, :],
+                sems.at[1 + n * pieces + q],
+            )
+            copy.start()
+            copies.append(copy)
+    taps_copy.wait()
+    taps = taps_ref[...].astype(jnp.float32)
+    taps = jnp.where(lax.rem(k, 2) == 0, taps[0:4, :], taps[4:8, :])
+    for g in range(4):
+        rows = [taps[g : g + 1, q * 128 : (q + 1) * 128] for q in range(pieces)]
+        block = jnp.concatenate(rows + rows, axis=0).astype(jnp.bfloat16)
+        for i in range(g * blocks // 4, (g + 1) * blocks // 4):
+            send_ref[i, 2 * span : 2 * span + 8, :] = block
     for copy in copies:
-        copy.start()
-    copies[0].wait()
-    taps = taps_ref[...].astype(jnp.float32)
-    taps = jnp.where(lax.rem(k, 2) == 0, taps[0:4, :], taps[4:8, :]).astype(jnp.bfloat16)
-    for i in range(blocks):
-        row = i * 4 // blocks
-        send_ref[i, 2 * per : 2 * per + 1, :] = taps[row : row + 1, :]
-    copies[1].wait()
-    copies[2].wait()
+        copy.wait()
 
 
 def pack(conv_input, output_grad, long_filter, blocks):
     channels, own = conv_input.shape
     share = channels // blocks
+    pieces = own // 128
     return pl.pallas_call(
         pack_kernel,
-        out_shape=pltpu.VMEM((blocks, 2 * share + 1, own), jnp.bfloat16),
+        out_shape=pltpu.VMEM((blocks, 2 * pieces * share + 8, 128), jnp.bfloat16),
         in_specs=[pl.BlockSpec(memory_space=pl.ANY)] * 3,
         out_specs=pl.BlockSpec(memory_space=pltpu.VMEM),
-        scratch_shapes=[pltpu.VMEM((8, own), jnp.bfloat16), pltpu.SemaphoreType.DMA((3,))],
+        scratch_shapes=[
+            pltpu.VMEM((8, own), jnp.bfloat16),
+            pltpu.SemaphoreType.DMA((1 + 2 * pieces,)),
+        ],
         name="pack",
     )(
         conv_input.reshape(blocks, share, own),
@@ -54,23 +67,29 @@
 
 
 def gradients_kernel(recv_ref, out_ref, og_ref, cit_ref, table_ref, skew_ref, acc_ref):
-    blocks, _, own = recv_ref.shape
+    blocks, height, _ = recv_ref.shape
     per = 32
+    pieces = (height - 8) // (2 * per)
+    span = pieces * per
+    own = pieces * 128
     tokens = blocks * own
     tiles = tokens // TILE
     rows = tiles * per
 
     ci = []
     for a in range(tiles):
-        j, lo = (a * TILE) // own, (a * TILE) % own
-        og_ref[a * per : (a + 1) * per, :] = recv_ref[j, per : 2 * per, lo : lo + TILE]
-        ci.append(recv_ref[j, 0:per, lo : lo + TILE])
+        j, q = divmod(2 * a, pieces)
+        left, right = slice(q * per, (q + 1) * per), slice((q + 1) * per, (q + 2) * per)
+        og_ref[a * per : (a + 1) * per, 0:128] = recv_ref[j, span + left.start : span + left.stop, :]
+        og_ref[a * per : (a + 1) * per, 128:256] = recv_ref[
+            j, span + right.start : span + right.stop, :
+        ]
+        ci.append(jnp.concatenate([recv_ref[j, left, :], recv_ref[j, right, :]], axis=1))
     og_ref[rows : 2 * rows, :] = jnp.zeros((rows, TILE), og_ref.dtype)
     cit_ref[...] = jnp.concatenate(ci, axis=0).T
 
-    taps = jnp.concatenate(
-        [recv_ref[j, 2 * per : 2 * per + 1, :].astype(jnp.float32) for j in range(blocks)], axis=1
-    )
+    taps = [recv_ref[j, 2 * span : 2 * span + 8, :].astype(jnp.float32) for j in range(blocks)]
+    taps = jnp.concatenate([x[q : q + 1, :] for x in taps for q in range(pieces)], axis=1)
     wide = jnp.broadcast_to(taps, (8, tokens))
     base = pltpu.roll(wide, 0, 1, stride=1, stride_axis=0)
     for t in range(0, 16, 2):
@@ -110,11 +129,13 @@
     lags = jnp.sum(folded, axis=0, keepdims=True)
     high = lags.astype(jnp.bfloat16).astype(jnp.float32)
     low = lags - high
-    row = lax.broadcasted_iota(jnp.int32, (8, own), 0)
     for j in range(blocks):
-        part = slice(j * own, (j + 1) * own)
-        packed = jnp.where(row == 0, high[:, part], jnp.where(row == 1, low[:, part], 0.0))
-        out_ref[j, per : per + 8, :] = packed.astype(jnp.bfloat16)
+        packed = [
+            part[:, at : at + 128]
+            for part in (high, low)
+            for at in range(j * own, (j + 1) * own, 128)
+        ]
+        out_ref[j, span : span + 8, :] = jnp.concatenate(packed, axis=0).astype(jnp.bfloat16)
 
     for d in range(tiles):
         live = rows - d * per
@@ -129,17 +150,20 @@
         else:
             acc_ref[0:live, :] = acc_ref[0:live, :] + term
     for a in range(tiles):
-        j, lo = (a * TILE) // own, (a * TILE) % own
-        out_ref[j, 0:per, lo : lo + TILE] = acc_ref[a * per : (a + 1) * per, :].astype(jnp.bfloat16)
+        j, q = divmod(2 * a, pieces)
+        done = acc_ref[a * per : (a + 1) * per, :].astype(jnp.bfloat16)
+        out_ref[j, q * per : (q + 1) * per, :] = done[:, 0:128]
+        out_ref[j, (q + 1) * per : (q + 2) * per, :] = done[:, 128:256]
 
 
 def gradients(recv):
-    blocks, _, own = recv.shape
-    tokens = blocks * own
+    blocks, height, _ = recv.shape
+    span = (height - 8) // 2
+    tokens = blocks * span * 128 // 32
     rows = tokens // TILE * 32
     return pl.pallas_call(
         gradients_kernel,
-        out_shape=pltpu.VMEM((blocks, 40, own), jnp.bfloat16),
+        out_shape=pltpu.VMEM((blocks, span + 8, 128), jnp.bfloat16),
         in_specs=[pl.BlockSpec(memory_space=pltpu.VMEM)],
         out_specs=pl.BlockSpec(memory_space=pltpu.VMEM),
         scratch_shapes=[
@@ -153,6 +177,81 @@
     )(pltpu.with_memory_space_constraint(recv, pltpu.VMEM))
 
 
+def spread_kernel(back_ref, out_ref):
+    blocks, height, _ = back_ref.shape
+    receivers, groups, own = out_ref.shape
+    pieces = own // 128
+    parts = [back_ref[i, height - 8 : height, :].astype(jnp.float32) for i in range(blocks)]
+    parts = [x[0:pieces, :] + x[pieces : 2 * pieces, :] for x in parts]
+    each = blocks // groups
+    sums = [sum(parts[g * each + 1 : (g + 1) * each], parts[g * each]) for g in range(groups)]
+    owned = jnp.concatenate(
+        [jnp.concatenate([x[q : q + 1, :] for x in sums], axis=0) for q in range(pieces)], axis=1
+    )
+    for n in range(receivers):
+        out_ref[n, :, :] = owned
+
+
+def spread(back, receivers, groups, own):
+    return pl.pallas_call(
+        spread_kernel,
+        out_shape=pltpu.VMEM((receivers, groups, own), jnp.float32),
+        in_specs=[pl.BlockSpec(memory_space=pltpu.VMEM)],
+        out_specs=pl.BlockSpec(memory_space=pltpu.VMEM),
+        name="spread",
+    )(back)
+
+
+def finish_kernel(back_ref, mine_ref, theirs_ref, ig_ref, fg_ref, both_ref, sems):
+    blocks, share, own = ig_ref.shape
+    senders, groups, _ = mine_ref.shape
+    copies = []
+    for q in range(own // 128):
+        copies.append(
+            pltpu.make_async_copy(
+                back_ref.at[:, q * share : (q + 1) * share, :],
+                ig_ref.at[:, :, q * 128 : (q + 1) * 128],
+                sems.at[q],
+            )
+        )
+    for copy in copies:
+        copy.start()
+    first = lax.rem(lax.axis_index("ch"), 2) == 0
+    half = senders // 2
+    for part in range(2):
+        for n in range(part * half, (part + 1) * half):
+            mine, theirs = mine_ref[n, :, :], theirs_ref[n, :, :]
+            both_ref[n, 0:groups, :] = jnp.where(first, mine, theirs)
+            both_ref[n, groups : 2 * groups, :] = jnp.where(first, theirs, mine)
+        copy = pltpu.make_async_copy(
+            both_ref.at[part * half : (part + 1) * half],
+            fg_ref.at[part * half : (part + 1) * half],
+            sems.at[own // 128 + part],
+        )
+        copy.start()
+        copies.append(copy)
+    for copy in copies:
+        copy.wait()
+
+
+def finish(back, mine, theirs, share, own):
+    senders, groups, _ = mine.shape
+    return pl.pallas_call(
+        finish_kernel,
+        out_shape=(
+            jax.ShapeDtypeStruct((back.shape[0], share, own), jnp.bfloat16),
+            jax.ShapeDtypeStruct((senders, 2 * groups, own), jnp.float32),
+        ),
+        in_specs=[pl.BlockSpec(memory_space=pltpu.VMEM)] * 3,
+        out_specs=(pl.BlockSpec(memory_space=pl.ANY),) * 2,
+        scratch_shapes=[
+            pltpu.VMEM((senders, 2 * groups, own), jnp.float32),
+            pltpu.SemaphoreType.DMA((own // 128 + 2,)),
+        ],
+        name="finish",
+    )(*(pltpu.with_memory_space_constraint(x, pltpu.VMEM) for x in (back, mine, theirs)))
+
+
 def per_device(conv_input, output_grad, long_filter):
     channels, own = conv_input.shape
     cycle = lax.axis_size("ctx")
@@ -161,26 +260,19 @@
     send = pack(conv_input, output_grad, long_filter, cycle)
     recv = lax.all_to_all(send, "ctx", 0, 0, tiled=True)
     back = lax.all_to_all(gradients(recv), "ctx", 0, 0, tiled=True)
-    input_grad = back[:, :share, :].reshape(channels, own)
-    parts = back[:, share : share + 2, :].astype(jnp.float32)
-    owned = jnp.sum(parts.reshape(groups_here, -1, own), axis=1)
+    back = pltpu.with_memory_space_constraint(back, pltpu.VMEM)
     peers = lax.axis_size("ch")
-    groups = [list(range(core, peers, 2)) for core in range(2)]
     mine = lax.all_to_all(
-        jnp.broadcast_to(owned[None], (peers // 2, groups_here, own)),
+        spread(back, peers // 2, groups_here, own),
         "ch",
         0,
         0,
-        axis_index_groups=groups,
+        axis_index_groups=[list(range(core, peers, 2)) for core in range(2)],
         tiled=True,
     )
     theirs = lax.ppermute(mine, "ch", [(k, k ^ 1) for k in range(peers)])
-    filter_grad = jnp.where(
-        lax.axis_index("ch") % 2 == 0,
-        jnp.concatenate([mine, theirs], axis=1),
-        jnp.concatenate([theirs, mine], axis=1),
-    )
-    return input_grad, filter_grad.reshape(G, own)
+    input_grad, filter_grad = finish(back, mine, theirs, share, own)
+    return input_grad.reshape(channels, own), filter_grad.reshape(G, own)
 
 
 def solution(mesh):

time: 55 us -> 54.6 us (level)
  Pallas kernels: 2.83 us -> 3.82 us
  other arithmetic: 0.87 us -> 0 us
  local copies, waits for them, and re-layouts: 0.76 us -> 0 us
  waiting for transfers between devices: 0.26 us -> 0.99 us
  blocking collectives: 44.8 us -> 44.2 us
    pallas_call x2 -> x4, Pallas kernels: 2.83 us -> 3.82 us  [the longest x1 1.78 us: gradients(): pl.pallas_call(gradients_kernel, out_shape=pltpu.VMEM((blocks, span + 8,...]
    select_n x1 -> x0, other arithmetic: 0.8 us -> none  [per_device(): jnp.where(lax.axis_index('ch') % 2 == 0, jnp.concatenate([mine, theirs],...]
    ppermute x1, waiting for transfers between devices: 0.26 us -> 0.99 us  [per_device(): theirs = lax.ppermute(mine, 'ch', [(k, k ^ 1) for k in range(peers)])]
    slice x1 -> x0, local copies, waits for them, and re-layouts: 0.72 us -> none  [per_device(): input_grad = back[:, :share, :].reshape(channels, own)]
  transfers between devices with their start and end apart: 1 -> 1, of which waited for: 1 -> 1; matrix products, arithmetic and copies ran while one was open for 1% -> 0% of each run, Pallas kernels for 0% -> 0%
where the time goes in v3:
time: 54.6 us; the launch traced here: 54.3 us
  blocking collectives  44.2 us (81%)
  starting transfers between devices  4.6 us (8%)
  Pallas kernels  3.82 us (7%)
  waiting for transfers between devices  0.99 us (2%)
  between operations  0.65 us (1%)
    all_to_all x1, blocking collectives, per_device(): recv = lax.all_to_all(send, 'ctx', 0, 0, tiled=True)  18.2 us
    all_to_all x1, blocking collectives, per_device(): lax.all_to_all(spread(back, peers // 2, groups_here, own), 'ch', 0, 0, ax...  15.6 us
    all_to_all x1, blocking collectives, per_device(): back = lax.all_to_all(gradients(recv), 'ctx', 0, 0, tiled=True)  10.4 us
    ppermute x1, starting transfers between devices, per_device(): theirs = lax.ppermute(mine, 'ch', [(k, k ^ 1) for k in range(peers)])  4.6 us
    pallas_call x1, Pallas kernels, gradients(): pl.pallas_call(gradients_kernel, out_shape=pltpu.VMEM((blocks, span + 8,...  1.78 us
    pallas_call x1, Pallas kernels, pack(): pl.pallas_call(pack_kernel, out_shape=pltpu.VMEM((blocks, 2 * pieces * sh...  1.19 us
  transfers between devices with their start and end apart: 1, of which 1 were waited for; matrix products, arithmetic and copies ran while one was open for 0% of the time, Pallas kernels for 0%

profile of v3, /device:TPU:1, one launch (start us, length us, event | category | flops | bytes accessed | tf_op | source)
XLA Modules:
  0.0 54.3 jit_solution(9937737737293485991)
XLA Ops:
  0.6 1.2 %pack.1 = bf16[8,264,128]{2,1,0:T(8,128)(2,1)S(1)} custom-call(bf16[8,32,512]{2,1,0:T(8,128)(2,1)} %bitcast.4, bf16[8,32,512]{2,1,0:T(8,128)(2,1)} %bitcast.5, bf16[128,512]{1,0:T(8,128)(2,1)} %filter_ref.1), custom_call_target="tpu_custom_call" | custom-call | tf_op jit(solution)/shard_map/pack/pallas_call | solution.py:47
  1.8 18.2 %all_to_all.15.recv_ref = bf16[8,264,128]{2,1,0:T(8,128)(2,1)S(1)} all-to-all(bf16[8,264,128]{2,1,0:T(8,128)(2,1)S(1)} %pack.1), channel_id=1, replica_groups=mesh['ctx'=8,'ch'=32] {'ctx'}, dimensions={0} | all-to-all | bytes 1081344 | tf_op jit(solution)/shard_map/all_to_all | solution.py:261
  20.0 1.8 %gradients.1 = bf16[8,136,128]{2,1,0:T(8,128)(2,1)S(1)} custom-call(bf16[8,264,128]{2,1,0:T(8,128)(2,1)S(1)} %all_to_all.15.recv_ref), custom_call_target="tpu_custom_call" | custom-call | tf_op jit(solution)/shard_map/gradients/pallas_call | solution.py:164
  21.8 10.4 %all_to_all.16.back_ref = bf16[8,136,128]{2,1,0:T(8,128)(2,1)S(1)} all-to-all(bf16[8,136,128]{2,1,0:T(8,128)(2,1)S(1)} %gradients.1), channel_id=1, replica_groups=mesh['ctx'=8,'ch'=32] {'ctx'}, dimensions={0} | all-to-all | bytes 557056 | tf_op jit(solution)/shard_map/all_to_all | solution.py:262
  32.2 15.6 %all_to_all.17.mine_ref = f32[16,4,512]{2,1,0:T(4,128)S(1)} all-to-all(f32[16,4,512]{2,1,0:T(4,128)S(1)} %spread.1), channel_id=1, replica_groups={{0,2,4,6,8,10,12,14,16,18,20,22,24,26,28,30},{1,3,5,7,9,11,13,15,17,19,..., dimensions={0} | all-to-all | bytes 262144 | tf_op jit(solution)/shard_map/all_to_all | solution.py:265
  47.9 4.6 %collective-permute-start = (f32[16,4,512]{2,1,0:T(4,128)S(1)}, f32[16,4,512]{2,1,0:T(4,128)S(1)}, u32[]{:S(2)}, u32[]{:S(2)}) collective-permute-start(f32[16,4,512]{2,1,0:T(4,128)S(1)} %all_to_all.17.mine_ref), channel_id=1, source_target_pairs={{0,1},{1,0},{2,3},{3,2},{4,5},{5,4},{6,7},{7,6},{8,9},{9,8},{10,11... | collective-permute-start | bytes 393224 | tf_op jit(solution)/shard_map/ppermute | solution.py:273
  52.5 1.0 %collective-permute-done.theirs_ref = f32[16,4,512]{2,1,0:T(4,128)S(1)} collective-permute-done((f32[16,4,512]{2,1,0:T(4,128)S(1)}, f32[16,4,512]{2,1,0:T(4,128)S(1)}, u32[]{:S(2)}, u32[]{:S(2)}) %collective-permute-start) | collective-permute-done | bytes 131104 | tf_op jit(solution)/shard_map/ppermute | solution.py:273
  53.5 0.8 %finish.1 = (bf16[8,32,512]{2,1,0:T(8,128)(2,1)}, f32[16,8,512]{2,1,0:T(8,128)}) custom-call(bf16[8,136,128]{2,1,0:T(8,128)(2,1)S(1)} %all_to_all.16.back_ref, f32[16,4,512]{2,1,0:T(4,128)S(1)} %all_to_all.17.mine_ref, f32[16,4,512]{2,1,0:T(4,128)S(1)} %collective-permute-done.theirs_ref), custom_call_target="tpu_custom_call" | custom-call | tf_op jit(solution)/shard_map/finish/pallas_call | solution.py:239
  (1 shorter events, 0.0 us)
Async XLA Ops:
  47.9 5.6 %collective-permute-start = (f32[16,4,512]{2,1,0:T(4,128)S(1)}, f32[16,4,512]{2,1,0:T(4,128)S(1)}, u32[]{:S(2)}, u32[]{:S(2)}) collective-permute-start(f32[16,4,512]{2,1,0:T(4,128)S(1)} %all_to_all.17.mine_ref), channel_id=1, source_target_pairs={{0,1},{1,0},{2,3},{3,2},{4,5},{5,4},{6,7},{7,6},{8,9},{9,8},{10,11... | collective-permute-start | bytes 393224 | tf_op jit(solution)/shard_map/ppermute | solution.py:273

commit v4 on v3

--- a/solution.py
+++ b/solution.py
@@ -8,6 +8,8 @@
 C = 8192
 G = 128
 TILE = 256
+FIRST_CTX = 6
+FIRST_CHIP = 4
 
 
 def pack_kernel(ci_ref, og_ref, filter_ref, send_ref, taps_ref, sems):
@@ -79,6 +81,7 @@
     ci = []
     for a in range(tiles):
         j, q = divmod(2 * a, pieces)
+        j = j ^ FIRST_CTX
         left, right = slice(q * per, (q + 1) * per), slice((q + 1) * per, (q + 2) * per)
         og_ref[a * per : (a + 1) * per, 0:128] = recv_ref[j, span + left.start : span + left.stop, :]
         og_ref[a * per : (a + 1) * per, 128:256] = recv_ref[
@@ -88,7 +91,10 @@
     og_ref[rows : 2 * rows, :] = jnp.zeros((rows, TILE), og_ref.dtype)
     cit_ref[...] = jnp.concatenate(ci, axis=0).T
 
-    taps = [recv_ref[j, 2 * span : 2 * span + 8, :].astype(jnp.float32) for j in range(blocks)]
+    taps = [
+        recv_ref[j ^ FIRST_CTX, 2 * span : 2 * span + 8, :].astype(jnp.float32)
+        for j in range(blocks)
+    ]
     taps = jnp.concatenate([x[q : q + 1, :] for x in taps for q in range(pieces)], axis=1)
     wide = jnp.broadcast_to(taps, (8, tokens))
     base = pltpu.roll(wide, 0, 1, stride=1, stride_axis=0)
@@ -135,7 +141,7 @@
             for part in (high, low)
             for at in range(j * own, (j + 1) * own, 128)
         ]
-        out_ref[j, span : span + 8, :] = jnp.concatenate(packed, axis=0).astype(jnp.bfloat16)
+        out_ref[j ^ FIRST_CTX, span : span + 8, :] = jnp.concatenate(packed, axis=0).astype(jnp.bfloat16)
 
     for d in range(tiles):
         live = rows - d * per
@@ -151,6 +157,7 @@
             acc_ref[0:live, :] = acc_ref[0:live, :] + term
     for a in range(tiles):
         j, q = divmod(2 * a, pieces)
+        j = j ^ FIRST_CTX
         done = acc_ref[a * per : (a + 1) * per, :].astype(jnp.bfloat16)
         out_ref[j, q * per : (q + 1) * per, :] = done[:, 0:128]
         out_ref[j, (q + 1) * per : (q + 2) * per, :] = done[:, 128:256]
@@ -220,7 +227,7 @@
     half = senders // 2
     for part in range(2):
         for n in range(part * half, (part + 1) * half):
-            mine, theirs = mine_ref[n, :, :], theirs_ref[n, :, :]
+            mine, theirs = mine_ref[n ^ FIRST_CHIP, :, :], theirs_ref[n ^ FIRST_CHIP, :, :]
             both_ref[n, 0:groups, :] = jnp.where(first, mine, theirs)
             both_ref[n, groups : 2 * groups, :] = jnp.where(first, theirs, mine)
         copy = pltpu.make_async_copy(
@@ -258,8 +265,9 @@
     share = channels // cycle
     groups_here = channels // (C // G)
     send = pack(conv_input, output_grad, long_filter, cycle)
-    recv = lax.all_to_all(send, "ctx", 0, 0, tiled=True)
-    back = lax.all_to_all(gradients(recv), "ctx", 0, 0, tiled=True)
+    ring = [[p ^ FIRST_CTX for p in range(cycle)]]
+    recv = lax.all_to_all(send, "ctx", 0, 0, axis_index_groups=ring, tiled=True)
+    back = lax.all_to_all(gradients(recv), "ctx", 0, 0, axis_index_groups=ring, tiled=True)
     back = pltpu.with_memory_space_constraint(back, pltpu.VMEM)
     peers = lax.axis_size("ch")
     mine = lax.all_to_all(
@@ -267,7 +275,9 @@
         "ch",
         0,
         0,
-        axis_index_groups=[list(range(core, peers, 2)) for core in range(2)],
+        axis_index_groups=[
+            [2 * (p ^ FIRST_CHIP) + core for p in range(peers // 2)] for core in range(2)
+        ],
         tiled=True,
     )
     theirs = lax.ppermute(mine, "ch", [(k, k ^ 1) for k in range(peers)])

time: 54.6 us -> 48.7 us (0.89)
  blocking collectives: 44.2 us -> 39.3 us
  starting transfers between devices: 4.6 us -> 3.67 us
    all_to_all x2, blocking collectives: 28.6 us -> 25 us  [the longest x1 15.4 us: per_device(): recv = lax.all_to_all(send, 'ctx', 0, 0, axis_index_groups=ring, tiled=True)]
    all_to_all x1, blocking collectives: 15.6 us -> 14.3 us  [per_device(): lax.all_to_all(spread(back, peers // 2, groups_here, own), 'ch', 0, 0, ax...]
    ppermute x1, starting transfers between devices: 4.6 us -> 3.67 us  [per_device(): theirs = lax.ppermute(mine, 'ch', [(k, k ^ 1) for k in range(peers)])]
where the time goes in v4:
time: 48.7 us; the launch traced here: 48.5 us
  blocking collectives  39.3 us (81%)
  Pallas kernels  3.82 us (8%)
  starting transfers between devices  3.67 us (8%)
  waiting for transfers between devices  0.99 us (2%)
  between operations  0.65 us (1%)
    all_to_all x1, blocking collectives, per_device(): recv = lax.all_to_all(send, 'ctx', 0, 0, axis_index_groups=ring, tiled=True)  15.4 us
    all_to_all x1, blocking collectives, per_device(): lax.all_to_all(spread(back, peers // 2, groups_here, own), 'ch', 0, 0, ax...  14.3 us
    all_to_all x1, blocking collectives, per_device(): lax.all_to_all(gradients(recv), 'ctx', 0, 0, axis_index_groups=ring, tile...  9.67 us
    ppermute x1, starting transfers between devices, per_device(): theirs = lax.ppermute(mine, 'ch', [(k, k ^ 1) for k in range(peers)])  3.67 us
    pallas_call x1, Pallas kernels, gradients(): pl.pallas_call(gradients_kernel, out_shape=pltpu.VMEM((blocks, span + 8,...  1.78 us
    pallas_call x1, Pallas kernels, pack(): pl.pallas_call(pack_kernel, out_shape=pltpu.VMEM((blocks, 2 * pieces * sh...  1.19 us
    ppermute x1, waiting for transfers between devices, per_device(): theirs = lax.ppermute(mine, 'ch', [(k, k ^ 1) for k in range(peers)])  0.99 us
  transfers between devices with their start and end apart: 1, of which 1 were waited for; matrix products, arithmetic and copies ran while one was open for 0% of the time, Pallas kernels for 0%

profile of v4, /device:TPU:1, one launch (start us, length us, event | category | flops | bytes accessed | tf_op | source)
XLA Modules:
  0.0 48.5 jit_solution(12850546871103491840)
XLA Ops:
  0.6 1.2 %pack.1 = bf16[8,264,128]{2,1,0:T(8,128)(2,1)S(1)} custom-call(bf16[8,32,512]{2,1,0:T(8,128)(2,1)} %bitcast.4, bf16[8,32,512]{2,1,0:T(8,128)(2,1)} %bitcast.5, bf16[128,512]{1,0:T(8,128)(2,1)} %filter_ref.1), custom_call_target="tpu_custom_call" | custom-call | tf_op jit(solution)/shard_map/pack/pallas_call | solution.py:49
  1.8 15.4 %all_to_all.15.recv_ref = bf16[8,264,128]{2,1,0:T(8,128)(2,1)S(1)} all-to-all(bf16[8,264,128]{2,1,0:T(8,128)(2,1)S(1)} %pack.1), channel_id=1, replica_groups={{192,224,128,160,64,96,0,32},{193,225,129,161,65,97,1,33},{194,226,130,..., dimensions={0} | all-to-all | bytes 1081344 | tf_op jit(solution)/shard_map/all_to_all | solution.py:269
  17.2 1.8 %gradients.1 = bf16[8,136,128]{2,1,0:T(8,128)(2,1)S(1)} custom-call(bf16[8,264,128]{2,1,0:T(8,128)(2,1)S(1)} %all_to_all.15.recv_ref), custom_call_target="tpu_custom_call" | custom-call | tf_op jit(solution)/shard_map/gradients/pallas_call | solution.py:171
  19.0 9.7 %all_to_all.16.back_ref = bf16[8,136,128]{2,1,0:T(8,128)(2,1)S(1)} all-to-all(bf16[8,136,128]{2,1,0:T(8,128)(2,1)S(1)} %gradients.1), channel_id=1, replica_groups={{192,224,128,160,64,96,0,32},{193,225,129,161,65,97,1,33},{194,226,130,..., dimensions={0} | all-to-all | bytes 557056 | tf_op jit(solution)/shard_map/all_to_all | solution.py:270
  28.7 14.3 %all_to_all.17.mine_ref = f32[16,4,512]{2,1,0:T(4,128)S(1)} all-to-all(f32[16,4,512]{2,1,0:T(4,128)S(1)} %spread.1), channel_id=1, replica_groups={{8,10,12,14,0,2,4,6,24,26,28,30,16,18,20,22},{9,11,13,15,1,3,5,7,25,27,..., dimensions={0} | all-to-all | bytes 262144 | tf_op jit(solution)/shard_map/all_to_all | solution.py:273
  43.0 3.7 %collective-permute-start = (f32[16,4,512]{2,1,0:T(4,128)S(1)}, f32[16,4,512]{2,1,0:T(4,128)S(1)}, u32[]{:S(2)}, u32[]{:S(2)}) collective-permute-start(f32[16,4,512]{2,1,0:T(4,128)S(1)} %all_to_all.17.mine_ref), channel_id=1, source_target_pairs={{0,1},{1,0},{2,3},{3,2},{4,5},{5,4},{6,7},{7,6},{8,9},{9,8},{10,11... | collective-permute-start | bytes 393224 | tf_op jit(solution)/shard_map/ppermute | solution.py:283
  46.6 1.0 %collective-permute-done.theirs_ref = f32[16,4,512]{2,1,0:T(4,128)S(1)} collective-permute-done((f32[16,4,512]{2,1,0:T(4,128)S(1)}, f32[16,4,512]{2,1,0:T(4,128)S(1)}, u32[]{:S(2)}, u32[]{:S(2)}) %collective-permute-start) | collective-permute-done | bytes 131104 | tf_op jit(solution)/shard_map/ppermute | solution.py:283
  47.6 0.8 %finish.1 = (bf16[8,32,512]{2,1,0:T(8,128)(2,1)}, f32[16,8,512]{2,1,0:T(8,128)}) custom-call(bf16[8,136,128]{2,1,0:T(8,128)(2,1)S(1)} %all_to_all.16.back_ref, f32[16,4,512]{2,1,0:T(4,128)S(1)} %all_to_all.17.mine_ref, f32[16,4,512]{2,1,0:T(4,128)S(1)} %collective-permute-done.theirs_ref), custom_call_target="tpu_custom_call" | custom-call | tf_op jit(solution)/shard_map/finish/pallas_call | solution.py:246
  (1 shorter events, 0.0 us)
Async XLA Ops:
  43.0 4.7 %collective-permute-start = (f32[16,4,512]{2,1,0:T(4,128)S(1)}, f32[16,4,512]{2,1,0:T(4,128)S(1)}, u32[]{:S(2)}, u32[]{:S(2)}) collective-permute-start(f32[16,4,512]{2,1,0:T(4,128)S(1)} %all_to_all.17.mine_ref), channel_id=1, source_target_pairs={{0,1},{1,0},{2,3},{3,2},{4,5},{5,4},{6,7},{7,6},{8,9},{9,8},{10,11... | collective-permute-start | bytes 393224 | tf_op jit(solution)/shard_map/ppermute | solution.py:283

commit v5 on v4

v5 whole, which is shorter than its diff:
```python
import jax
import jax.numpy as jnp
from jax import lax
from jax.experimental import pallas as pl
from jax.experimental.pallas import tpu as pltpu
from jax.sharding import PartitionSpec as P

C = 8192
G = 128
TILE = 256
FIRST_CTX = 6
FIRST_CHIP = 4
CTX_SLOT = [j ^ FIRST_CTX for j in range(8)]


def pack_kernel(ci_ref, og_ref, filter_ref, send_ref, taps_ref, sems):
    blocks, span, _ = ci_ref.shape
    pieces = filter_ref.shape[1] // 128
    k = lax.axis_index("ch")
    at = pl.multiple_of(8 * lax.div(k, 2), 8)
    copies = [
        pltpu.make_async_copy(filter_ref.at[pl.ds(at, 8), :], taps_ref, sems.at[0]),
        pltpu.make_async_copy(ci_ref, send_ref.at[:, 0:span, :], sems.at[1]),
        pltpu.make_async_copy(og_ref, send_ref.at[:, span : 2 * span, :], sems.at[2]),
    ]
    for copy in copies:
        copy.start()
    copies[0].wait()
    taps = taps_ref[...].astype(jnp.float32)
    taps = jnp.where(lax.rem(k, 2) == 0, taps[0:4, :], taps[4:8, :])
    for g in range(4):
        rows = [taps[g : g + 1, q * 128 : (q + 1) * 128] for q in range(pieces)]
        block = jnp.concatenate(rows + rows, axis=0).astype(jnp.bfloat16)
        for i in range(g * blocks // 4, (g + 1) * blocks // 4):
            send_ref[i, 2 * span : 2 * span + 8, :] = block
    copies[1].wait()
    copies[2].wait()


def tiles_of(x, blocks):
    channels, own = x.shape
    x = x.reshape(channels // 8, 8, own // 128, 128).transpose(0, 2, 1, 3)
    return x.reshape(blocks, channels * own // (128 * blocks), 128)


def pack(conv_input, output_grad, long_filter, blocks):
    channels, own = conv_input.shape
    span = channels * own // (128 * blocks)
    return pl.pallas_call(
        pack_kernel,
        out_shape=pltpu.VMEM((blocks, 2 * span + 8, 128), jnp.bfloat16),
        in_specs=[pl.BlockSpec(memory_space=pl.ANY)] * 3,
        out_specs=pl.BlockSpec(memory_space=pltpu.VMEM),
        scratch_shapes=[pltpu.VMEM((8, own), jnp.bfloat16), pltpu.SemaphoreType.DMA((3,))],
        name="pack",
    )(tiles_of(conv_input, blocks), tiles_of(output_grad, blocks), long_filter)


def roll_left(x, amount):
    lanes = x.shape[1]
    return x if amount == 0 else pltpu.roll(x, lanes - amount, 1)


def gradients_kernel(
    recv_ref, out_ref, og_ref, pair_ref, cit_ref, table_ref, skew_ref, acc_ref
):
    blocks, height, _ = recv_ref.shape
    per = 32
    pieces = (height - 8) // (2 * per)
    span = pieces * per
    own = pieces * 128
    tokens = blocks * own
    tiles = tokens // TILE
    rows = tiles * per
    small = tokens // 128

    def piece(base, a, r):
        j, q = divmod(a, pieces)
        at = base + (r * pieces + q) * 8
        return recv_ref[CTX_SLOT[j], at : at + 8, :]

    for a in range(small):
        for r in range(per // 8):
            x = piece(span, a, r)
            to = slice(a * per + r * 8, a * per + r * 8 + 8)
            pair_ref[to, 0:128] = x
            if a > 0:
                pair_ref[to.start - per : to.stop - per, 128:256] = x
            to = slice(a // 2 * per + r * 8, a // 2 * per + r * 8 + 8)
            og_ref[to, (a % 2) * 128 : (a % 2) * 128 + 128] = x
    pair_ref[(small - 1) * per : small * per, 128:256] = jnp.zeros((per, 128), pair_ref.dtype)
    pair_ref[small * per :, :] = jnp.zeros((pair_ref.shape[0] - small * per, TILE), pair_ref.dtype)
    for m in range(small // 8):
        ci = [piece(0, a, r) for a in range(8 * m, 8 * m + 8) for r in range(per // 8)]
        cit_ref[m * 128 : (m + 1) * 128, :] = jnp.concatenate(ci, axis=0).T

    taps = [
        recv_ref[CTX_SLOT[j], 2 * span : 2 * span + 8, :].astype(jnp.float32)
        for j in range(blocks)
    ]
    taps = jnp.concatenate([x[q : q + 1, :] for x in taps for q in range(pieces)], axis=1)
    wide = jnp.broadcast_to(taps, (8, tokens))
    base = pltpu.roll(wide, 0, 1, stride=1, stride_axis=0)
    for t in range(0, 16, 2):
        pair = jnp.concatenate(
            [base if t == 0 else pltpu.roll(base, 8 * t, 1), pltpu.roll(base, 8 * t + 8, 1)], axis=0
        )
        u = 8 * t + lax.broadcasted_iota(jnp.int32, (16, 128), 0)
        first = jnp.where(lax.broadcasted_iota(jnp.int32, (16, 128), 1) >= u, pair[:, 0:128], 0.0)
        pair = jnp.concatenate([first, pair[:, 128:]], axis=1).astype(jnp.bfloat16)
        table_ref[8 * t : 8 * t + 16, :] = pair
        table_ref[128 + 8 * t : 128 + 8 * t + 16, 128:] = pair[:, : tokens - 128]
        table_ref[128 + 8 * t : 128 + 8 * t + 16, 0:128] = jnp.zeros((16, 128), jnp.bfloat16)

    for n in range(tiles):
        parts = n // 4 + 1
        cross = jnp.dot(
            cit_ref[0 : parts * 128, :],
            pair_ref[n * 2 * per : n * 2 * per + 8 * per, :],
            preferred_element_type=jnp.float32,
        )
        for m in range(parts):
            term = cross[m * 128 : (m + 1) * 128, :]
            d = n - 4 * m
            if d == 0:
                u = lax.broadcasted_iota(jnp.int32, (128, TILE), 0)
                v = lax.broadcasted_iota(jnp.int32, (128, TILE), 1)
                term = jnp.where(v >= u, term, 0.0)
            to = slice(d * TILE, (d + 1) * TILE)
            skew_ref[:, to] = term if m == 0 else skew_ref[:, to] + term
    folded = skew_ref[0:8, :]
    for t in range(1, 16):
        folded = folded + roll_left(skew_ref[8 * t : 8 * t + 8, :], 8 * t)
    r = lax.broadcasted_iota(jnp.int32, folded.shape, 0)
    for bit in (1, 2, 4):
        folded = jnp.where((r & bit) > 0, roll_left(folded, bit), folded)
    lags = jnp.sum(folded, axis=0, keepdims=True)
    high = lags.astype(jnp.bfloat16).astype(jnp.float32)
    low = lags - high
    for j in range(blocks):
        packed = [
            part[:, at : at + 128]
            for part in (high, low)
            for at in range(j * own, (j + 1) * own, 128)
        ]
        out_ref[CTX_SLOT[j], span : span + 8, :] = jnp.concatenate(packed, axis=0).astype(jnp.bfloat16)

    for d in range(tiles):
        live = rows - d * per
        term = lax.dot_general(
            og_ref[d * per : rows, :],
            table_ref[:, d * TILE : (d + 1) * TILE],
            (((1,), (1,)), ((), ())),
            preferred_element_type=jnp.float32,
        )
        if d == 0:
            acc_ref[...] = term
        else:
            acc_ref[0:live, :] = acc_ref[0:live, :] + term
    for a in range(tiles):
        j, q = divmod(2 * a, pieces)
        done = acc_ref[a * per : (a + 1) * per, :].astype(jnp.bfloat16)
        for r in range(per // 8):
            at = (r * pieces + q) * 8
            out_ref[CTX_SLOT[j], at : at + 8, :] = done[r * 8 : r * 8 + 8, 0:128]
            out_ref[CTX_SLOT[j], at + 8 : at + 16, :] = done[r * 8 : r * 8 + 8, 128:256]


def gradients(recv):
    blocks, height, _ = recv.shape
    span = (height - 8) // 2
    tokens = blocks * span * 128 // 32
    rows = tokens // TILE * 32
    return pl.pallas_call(
        gradients_kernel,
        out_shape=pltpu.VMEM((blocks, span + 8, 128), jnp.bfloat16),
        in_specs=[pl.BlockSpec(memory_space=pltpu.VMEM)],
        out_specs=pl.BlockSpec(memory_space=pltpu.VMEM),
        scratch_shapes=[
            pltpu.VMEM((rows, TILE), jnp.bfloat16),
            pltpu.VMEM((2 * rows + 192, TILE), jnp.bfloat16),
            pltpu.VMEM((rows, TILE), jnp.bfloat16),
            pltpu.VMEM((TILE, tokens), jnp.bfloat16),
            pltpu.VMEM((128, tokens), jnp.float32),
            pltpu.VMEM((rows, TILE), jnp.float32),
        ],
        name="gradients",
    )(pltpu.with_memory_space_constraint(recv, pltpu.VMEM))


def spread_kernel(back_ref, out_ref):
    blocks, height, _ = back_ref.shape
    receivers, groups, own = out_ref.shape
    pieces = own // 128
    parts = [back_ref[i, height - 8 : height, :].astype(jnp.float32) for i in range(blocks)]
    parts = [x[0:pieces, :] + x[pieces : 2 * pieces, :] for x in parts]
    each = blocks // groups
    sums = [sum(parts[g * each + 1 : (g + 1) * each], parts[g * each]) for g in range(groups)]
    owned = jnp.concatenate(
        [jnp.concatenate([x[q : q + 1, :] for x in sums], axis=0) for q in range(pieces)], axis=1
    )
    for n in range(receivers):
        out_ref[n, :, :] = owned


def spread(back, receivers, groups, own):
    return pl.pallas_call(
        spread_kernel,
        out_shape=pltpu.VMEM((receivers, groups, own), jnp.float32),
        in_specs=[pl.BlockSpec(memory_space=pltpu.VMEM)],
        out_specs=pl.BlockSpec(memory_space=pltpu.VMEM),
        name="spread",
    )(back)


def finish_kernel(back_ref, mine_ref, theirs_ref, ig_ref, fg_ref, both_ref, sems):
    span = ig_ref.shape[1]
    senders, groups, own = mine_ref.shape
    copies = [pltpu.make_async_copy(back_ref.at[:, 0:span, :], ig_ref, sems.at[0])]
    copies[0].start()
    first = lax.rem(lax.axis_index("ch"), 2) == 0
    half = senders // 2
    for part in range(2):
        for n in range(part * half, (part + 1) * half):
            mine, theirs = mine_ref[n ^ FIRST_CHIP, :, :], theirs_ref[n ^ FIRST_CHIP, :, :]
            both_ref[n, 0:groups, :] = jnp.where(first, mine, theirs)
            both_ref[n, groups : 2 * groups, :] = jnp.where(first, theirs, mine)
        copy = pltpu.make_async_copy(
            both_ref.at[part * half : (part + 1) * half],
            fg_ref.at[part * half : (part + 1) * half],
            sems.at[1 + part],
        )
        copy.start()
        copies.append(copy)
    for copy in copies:
        copy.wait()


def finish(back, mine, theirs):
    senders, groups, own = mine.shape
    return pl.pallas_call(
        finish_kernel,
        out_shape=(
            jax.ShapeDtypeStruct((back.shape[0], back.shape[1] - 8, 128), jnp.bfloat16),
            jax.ShapeDtypeStruct((senders, 2 * groups, own), jnp.float32),
        ),
        in_specs=[pl.BlockSpec(memory_space=pltpu.VMEM)] * 3,
        out_specs=(pl.BlockSpec(memory_space=pl.ANY),) * 2,
        scratch_shapes=[
            pltpu.VMEM((senders, 2 * groups, own), jnp.float32),
            pltpu.SemaphoreType.DMA((3,)),
        ],
        name="finish",
    )(*(pltpu.with_memory_space_constraint(x, pltpu.VMEM) for x in (back, mine, theirs)))


def per_device(conv_input, output_grad, long_filter):
    channels, own = conv_input.shape
    cycle = lax.axis_size("ctx")
    groups_here = channels // (C // G)
    send = pack(conv_input, output_grad, long_filter, cycle)
    ring = [[p ^ FIRST_CTX for p in range(cycle)]]
    recv = lax.all_to_all(send, "ctx", 0, 0, axis_index_groups=ring, tiled=True)
    back = lax.all_to_all(gradients(recv), "ctx", 0, 0, axis_index_groups=ring, tiled=True)
    back = pltpu.with_memory_space_constraint(back, pltpu.VMEM)
    peers = lax.axis_size("ch")
    mine = lax.all_to_all(
        spread(back, peers // 2, groups_here, own),
        "ch",
        0,
        0,
        axis_index_groups=[
            [2 * (p ^ FIRST_CHIP) + core for p in range(peers // 2)] for core in range(2)
        ],
        tiled=True,
    )
    theirs = lax.ppermute(mine, "ch", [(k, k ^ 1) for k in range(peers)])
    input_grad, filter_grad = finish(back, mine, theirs)
    input_grad = input_grad.reshape(channels // 8, own // 128, 8, 128).transpose(0, 2, 1, 3)
    return input_grad.reshape(channels, own), filter_grad.reshape(G, own)


def solution(mesh):
    in_specs = (P("ch", "ctx"), P("ch", "ctx"), P(None, "ctx"))
    out_specs = (P("ch", "ctx"), P(None, "ctx"))
    return jax.shard_map(
        per_device, mesh=mesh, in_specs=in_specs, out_specs=out_specs, check_vma=False
    )
```

time: 48.7 us -> 48.5 us (level)
  no operation moved by 1% of the time
where the time goes in v5:
time: 48.5 us; the launch traced here: 48.3 us
  blocking collectives  39.3 us (81%)
  starting transfers between devices  3.67 us (8%)
  Pallas kernels  3.63 us (7%)
  waiting for transfers between devices  0.99 us (2%)
  between operations  0.65 us (1%)
    all_to_all x1, blocking collectives, per_device(): recv = lax.all_to_all(send, 'ctx', 0, 0, axis_index_groups=ring, tiled=True)  15.4 us
    all_to_all x1, blocking collectives, per_device(): lax.all_to_all(spread(back, peers // 2, groups_here, own), 'ch', 0, 0, ax...  14.3 us
    all_to_all x1, blocking collectives, per_device(): lax.all_to_all(gradients(recv), 'ctx', 0, 0, axis_index_groups=ring, tile...  9.67 us
    ppermute x1, starting transfers between devices, per_device(): theirs = lax.ppermute(mine, 'ch', [(k, k ^ 1) for k in range(peers)])  3.67 us
    pallas_call x1, Pallas kernels, gradients(): pl.pallas_call(gradients_kernel, out_shape=pltpu.VMEM((blocks, span + 8,...  1.72 us
    pallas_call x1, Pallas kernels, pack(): pl.pallas_call(pack_kernel, out_shape=pltpu.VMEM((blocks, 2 * span + 8, 1...  1.08 us
    ppermute x1, waiting for transfers between devices, per_device(): theirs = lax.ppermute(mine, 'ch', [(k, k ^ 1) for k in range(peers)])  0.99 us
  transfers between devices with their start and end apart: 1, of which 1 were waited for; matrix products, arithmetic and copies ran while one was open for 0% of the time, Pallas kernels for 0%

profile of v5, /device:TPU:1, one launch (start us, length us, event | category | flops | bytes accessed | tf_op | source)
XLA Modules:
  0.0 48.3 jit_solution(14690608703274173990)
XLA Ops:
  0.6 1.1 %pack.1 = bf16[8,264,128]{2,1,0:T(8,128)(2,1)S(1)} custom-call(bf16[8,128,128]{2,1,0:T(8,128)(2,1)} %bitcast.16, bf16[8,128,128]{2,1,0:T(8,128)(2,1)} %bitcast.17, bf16[128,512]{1,0:T(8,128)(2,1)} %filter_ref.1), custom_call_target="tpu_custom_call" | custom-call | tf_op jit(solution)/shard_map/pack/pallas_call | solution.py:49
  1.7 15.4 %all_to_all.15.recv_ref = bf16[8,264,128]{2,1,0:T(8,128)(2,1)S(1)} all-to-all(bf16[8,264,128]{2,1,0:T(8,128)(2,1)S(1)} %pack.1), channel_id=1, replica_groups={{192,224,128,160,64,96,0,32},{193,225,129,161,65,97,1,33},{194,226,130,..., dimensions={0} | all-to-all | bytes 1081344 | tf_op jit(solution)/shard_map/all_to_all | solution.py:263
  17.1 1.7 %gradients.1 = bf16[8,136,128]{2,1,0:T(8,128)(2,1)S(1)} custom-call(bf16[8,264,128]{2,1,0:T(8,128)(2,1)S(1)} %all_to_all.15.recv_ref), custom_call_target="tpu_custom_call" | custom-call | tf_op jit(solution)/shard_map/gradients/pallas_call | solution.py:174
  18.8 9.7 %all_to_all.16.back_ref = bf16[8,136,128]{2,1,0:T(8,128)(2,1)S(1)} all-to-all(bf16[8,136,128]{2,1,0:T(8,128)(2,1)S(1)} %gradients.1), channel_id=1, replica_groups={{192,224,128,160,64,96,0,32},{193,225,129,161,65,97,1,33},{194,226,130,..., dimensions={0} | all-to-all | bytes 557056 | tf_op jit(solution)/shard_map/all_to_all | solution.py:264
  28.5 14.3 %all_to_all.17.mine_ref = f32[16,4,512]{2,1,0:T(4,128)S(1)} all-to-all(f32[16,4,512]{2,1,0:T(4,128)S(1)} %spread.1), channel_id=1, replica_groups={{8,10,12,14,0,2,4,6,24,26,28,30,16,18,20,22},{9,11,13,15,1,3,5,7,25,27,..., dimensions={0} | all-to-all | bytes 262144 | tf_op jit(solution)/shard_map/all_to_all | solution.py:267
  42.8 3.7 %collective-permute-start = (f32[16,4,512]{2,1,0:T(4,128)S(1)}, f32[16,4,512]{2,1,0:T(4,128)S(1)}, u32[]{:S(2)}, u32[]{:S(2)}) collective-permute-start(f32[16,4,512]{2,1,0:T(4,128)S(1)} %all_to_all.17.mine_ref), channel_id=1, source_target_pairs={{0,1},{1,0},{2,3},{3,2},{4,5},{5,4},{6,7},{7,6},{8,9},{9,8},{10,11... | collective-permute-start | bytes 393224 | tf_op jit(solution)/shard_map/ppermute | solution.py:277
  46.5 1.0 %collective-permute-done.theirs_ref = f32[16,4,512]{2,1,0:T(4,128)S(1)} collective-permute-done((f32[16,4,512]{2,1,0:T(4,128)S(1)}, f32[16,4,512]{2,1,0:T(4,128)S(1)}, u32[]{:S(2)}, u32[]{:S(2)}) %collective-permute-start) | collective-permute-done | bytes 131104 | tf_op jit(solution)/shard_map/ppermute | solution.py:277
  47.5 0.8 %finish.1 = (bf16[8,128,128]{2,1,0:T(8,128)(2,1)}, f32[16,8,512]{2,1,0:T(8,128)}) custom-call(bf16[8,136,128]{2,1,0:T(8,128)(2,1)S(1)} %all_to_all.16.back_ref, f32[16,4,512]{2,1,0:T(4,128)S(1)} %all_to_all.17.mine_ref, f32[16,4,512]{2,1,0:T(4,128)S(1)} %collective-permute-done.theirs_ref), custom_call_target="tpu_custom_call" | custom-call | tf_op jit(solution)/shard_map/finish/pallas_call | solution.py:241
  (1 shorter events, 0.0 us)
Async XLA Ops:
  42.8 4.7 %collective-permute-start = (f32[16,4,512]{2,1,0:T(4,128)S(1)}, f32[16,4,512]{2,1,0:T(4,128)S(1)}, u32[]{:S(2)}, u32[]{:S(2)}) collective-permute-start(f32[16,4,512]{2,1,0:T(4,128)S(1)} %all_to_all.17.mine_ref), channel_id=1, source_target_pairs={{0,1},{1,0},{2,3},{3,2},{4,5},{5,4},{6,7},{7,6},{8,9},{9,8},{10,11... | collective-permute-start | bytes 393224 | tf_op jit(solution)/shard_map/ppermute | solution.py:277

commit v6 on v5

--- a/solution.py
+++ b/solution.py
@@ -8,6 +8,7 @@
 C = 8192
 G = 128
 TILE = 256
+CHUNK = 512
 FIRST_CTX = 6
 FIRST_CHIP = 4
 CTX_SLOT = [j ^ FIRST_CTX for j in range(8)]
@@ -101,16 +102,25 @@
     taps = jnp.concatenate([x[q : q + 1, :] for x in taps for q in range(pieces)], axis=1)
     wide = jnp.broadcast_to(taps, (8, tokens))
     base = pltpu.roll(wide, 0, 1, stride=1, stride_axis=0)
-    for t in range(0, 16, 2):
-        pair = jnp.concatenate(
-            [base if t == 0 else pltpu.roll(base, 8 * t, 1), pltpu.roll(base, 8 * t + 8, 1)], axis=0
-        )
-        u = 8 * t + lax.broadcasted_iota(jnp.int32, (16, 128), 0)
-        first = jnp.where(lax.broadcasted_iota(jnp.int32, (16, 128), 1) >= u, pair[:, 0:128], 0.0)
-        pair = jnp.concatenate([first, pair[:, 128:]], axis=1).astype(jnp.bfloat16)
-        table_ref[8 * t : 8 * t + 16, :] = pair
-        table_ref[128 + 8 * t : 128 + 8 * t + 16, 128:] = pair[:, : tokens - 128]
-        table_ref[128 + 8 * t : 128 + 8 * t + 16, 0:128] = jnp.zeros((16, 128), jnp.bfloat16)
+    for lo in range(0, tokens, CHUNK):
+        before = (lo - 128) % tokens
+        wide = jnp.concatenate([base[:, before : before + 128], base[:, lo : lo + CHUNK]], axis=1)
+        for t in range(0, 16, 2):
+            pair = [wide if t == 0 else pltpu.roll(wide, 8 * t, 1), pltpu.roll(wide, 8 * t + 8, 1)]
+            pair = jnp.concatenate(pair, axis=0)[:, 128:]
+            if lo == 0:
+                u = 8 * t + lax.broadcasted_iota(jnp.int32, (16, 128), 0)
+                v = lax.broadcasted_iota(jnp.int32, (16, 128), 1)
+                first = jnp.where(v >= u, pair[:, 0:128], 0.0)
+                pair = jnp.concatenate([first, pair[:, 128:]], axis=1)
+            pair = pair.astype(jnp.bfloat16)
+            row = slice(8 * t, 8 * t + 16)
+            table_ref[row, lo : lo + CHUNK] = pair
+            row = slice(128 + 8 * t, 128 + 8 * t + 16)
+            stop = min(lo + CHUNK + 128, tokens)
+            table_ref[row, lo + 128 : stop] = pair[:, : stop - lo - 128]
+            if lo == 0:
+                table_ref[row, 0:128] = jnp.zeros((16, 128), jnp.bfloat16)
 
     for n in range(tiles):
         parts = n // 4 + 1
@@ -128,9 +138,16 @@
                 term = jnp.where(v >= u, term, 0.0)
             to = slice(d * TILE, (d + 1) * TILE)
             skew_ref[:, to] = term if m == 0 else skew_ref[:, to] + term
-    folded = skew_ref[0:8, :]
-    for t in range(1, 16):
-        folded = folded + roll_left(skew_ref[8 * t : 8 * t + 8, :], 8 * t)
+    folded = []
+    for lo in range(0, tokens, CHUNK):
+        after = (lo + CHUNK) % tokens
+        total = skew_ref[0:8, lo : lo + CHUNK]
+        for t in range(1, 16):
+            row = slice(8 * t, 8 * t + 8)
+            wide = [skew_ref[row, lo : lo + CHUNK], skew_ref[row, after : after + 128]]
+            total = total + roll_left(jnp.concatenate(wide, axis=1), 8 * t)[:, 0:CHUNK]
+        folded.append(total)
+    folded = jnp.concatenate(folded, axis=1)
     r = lax.broadcasted_iota(jnp.int32, folded.shape, 0)
     for bit in (1, 2, 4):
         folded = jnp.where((r & bit) > 0, roll_left(folded, bit), folded)

time: 48.5 us -> 48.5 us (level)
  no operation moved by 1% of the time
where the time goes in v6:
time: 48.5 us; the launch traced here: 48.3 us
  blocking collectives  39.3 us (81%)
  starting transfers between devices  3.67 us (8%)
  Pallas kernels  3.62 us (7%)
  waiting for transfers between devices  0.99 us (2%)
  between operations  0.65 us (1%)
    all_to_all x1, blocking collectives, per_device(): recv = lax.all_to_all(send, 'ctx', 0, 0, axis_index_groups=ring, tiled=True)  15.4 us
    all_to_all x1, blocking collectives, per_device(): lax.all_to_all(spread(back, peers // 2, groups_here, own), 'ch', 0, 0, ax...  14.3 us
    all_to_all x1, blocking collectives, per_device(): lax.all_to_all(gradients(recv), 'ctx', 0, 0, axis_index_groups=ring, tile...  9.67 us
    ppermute x1, starting transfers between devices, per_device(): theirs = lax.ppermute(mine, 'ch', [(k, k ^ 1) for k in range(peers)])  3.67 us
    pallas_call x1, Pallas kernels, gradients(): pl.pallas_call(gradients_kernel, out_shape=pltpu.VMEM((blocks, span + 8,...  1.71 us
    pallas_call x1, Pallas kernels, pack(): pl.pallas_call(pack_kernel, out_shape=pltpu.VMEM((blocks, 2 * span + 8, 1...  1.08 us
    ppermute x1, waiting for transfers between devices, per_device(): theirs = lax.ppermute(mine, 'ch', [(k, k ^ 1) for k in range(peers)])  0.99 us
  transfers between devices with their start and end apart: 1, of which 1 were waited for; matrix products, arithmetic and copies ran while one was open for 0% of the time, Pallas kernels for 0%

profile of v6, /device:TPU:1, one launch (start us, length us, event | category | flops | bytes accessed | tf_op | source)
XLA Modules:
  0.0 48.3 jit_solution(4822060904961394571)
XLA Ops:
  0.6 1.1 %pack.1 = bf16[8,264,128]{2,1,0:T(8,128)(2,1)S(1)} custom-call(bf16[8,128,128]{2,1,0:T(8,128)(2,1)} %bitcast.16, bf16[8,128,128]{2,1,0:T(8,128)(2,1)} %bitcast.17, bf16[128,512]{1,0:T(8,128)(2,1)} %filter_ref.1), custom_call_target="tpu_custom_call" | custom-call | tf_op jit(solution)/shard_map/pack/pallas_call | solution.py:50
  1.7 15.4 %all_to_all.15.recv_ref = bf16[8,264,128]{2,1,0:T(8,128)(2,1)S(1)} all-to-all(bf16[8,264,128]{2,1,0:T(8,128)(2,1)S(1)} %pack.1), channel_id=1, replica_groups={{192,224,128,160,64,96,0,32},{193,225,129,161,65,97,1,33},{194,226,130,..., dimensions={0} | all-to-all | bytes 1081344 | tf_op jit(solution)/shard_map/all_to_all | solution.py:280
  17.1 1.7 %gradients.1 = bf16[8,136,128]{2,1,0:T(8,128)(2,1)S(1)} custom-call(bf16[8,264,128]{2,1,0:T(8,128)(2,1)S(1)} %all_to_all.15.recv_ref), custom_call_target="tpu_custom_call" | custom-call | tf_op jit(solution)/shard_map/gradients/pallas_call | solution.py:191
  18.8 9.7 %all_to_all.16.back_ref = bf16[8,136,128]{2,1,0:T(8,128)(2,1)S(1)} all-to-all(bf16[8,136,128]{2,1,0:T(8,128)(2,1)S(1)} %gradients.1), channel_id=1, replica_groups={{192,224,128,160,64,96,0,32},{193,225,129,161,65,97,1,33},{194,226,130,..., dimensions={0} | all-to-all | bytes 557056 | tf_op jit(solution)/shard_map/all_to_all | solution.py:281
  28.5 14.3 %all_to_all.17.mine_ref = f32[16,4,512]{2,1,0:T(4,128)S(1)} all-to-all(f32[16,4,512]{2,1,0:T(4,128)S(1)} %spread.1), channel_id=1, replica_groups={{8,10,12,14,0,2,4,6,24,26,28,30,16,18,20,22},{9,11,13,15,1,3,5,7,25,27,..., dimensions={0} | all-to-all | bytes 262144 | tf_op jit(solution)/shard_map/all_to_all | solution.py:284
  42.8 3.7 %collective-permute-start = (f32[16,4,512]{2,1,0:T(4,128)S(1)}, f32[16,4,512]{2,1,0:T(4,128)S(1)}, u32[]{:S(2)}, u32[]{:S(2)}) collective-permute-start(f32[16,4,512]{2,1,0:T(4,128)S(1)} %all_to_all.17.mine_ref), channel_id=1, source_target_pairs={{0,1},{1,0},{2,3},{3,2},{4,5},{5,4},{6,7},{7,6},{8,9},{9,8},{10,11... | collective-permute-start | bytes 393224 | tf_op jit(solution)/shard_map/ppermute | solution.py:294
  46.5 1.0 %collective-permute-done.theirs_ref = f32[16,4,512]{2,1,0:T(4,128)S(1)} collective-permute-done((f32[16,4,512]{2,1,0:T(4,128)S(1)}, f32[16,4,512]{2,1,0:T(4,128)S(1)}, u32[]{:S(2)}, u32[]{:S(2)}) %collective-permute-start) | collective-permute-done | bytes 131104 | tf_op jit(solution)/shard_map/ppermute | solution.py:294
  47.5 0.8 %finish.1 = (bf16[8,128,128]{2,1,0:T(8,128)(2,1)}, f32[16,8,512]{2,1,0:T(8,128)}) custom-call(bf16[8,136,128]{2,1,0:T(8,128)(2,1)S(1)} %all_to_all.16.back_ref, f32[16,4,512]{2,1,0:T(4,128)S(1)} %all_to_all.17.mine_ref, f32[16,4,512]{2,1,0:T(4,128)S(1)} %collective-permute-done.theirs_ref), custom_call_target="tpu_custom_call" | custom-call | tf_op jit(solution)/shard_map/finish/pallas_call | solution.py:258
  (1 shorter events, 0.0 us)
Async XLA Ops:
  42.8 4.7 %collective-permute-start = (f32[16,4,512]{2,1,0:T(4,128)S(1)}, f32[16,4,512]{2,1,0:T(4,128)S(1)}, u32[]{:S(2)}, u32[]{:S(2)}) collective-permute-start(f32[16,4,512]{2,1,0:T(4,128)S(1)} %all_to_all.17.mine_ref), channel_id=1, source_target_pairs={{0,1},{1,0},{2,3},{3,2},{4,5},{5,4},{6,7},{7,6},{8,9},{9,8},{10,11... | collective-permute-start | bytes 393224 | tf_op jit(solution)/shard_map/ppermute | solution.py:294

commit v7 on v6

--- a/solution.py
+++ b/solution.py
@@ -174,7 +174,7 @@
             acc_ref[...] = term
         else:
             acc_ref[0:live, :] = acc_ref[0:live, :] + term
-    for a in range(tiles):
+        a = tiles - 1 - d
         j, q = divmod(2 * a, pieces)
         done = acc_ref[a * per : (a + 1) * per, :].astype(jnp.bfloat16)
         for r in range(per // 8):

time: 48.5 us -> 48.5 us (level)
  no operation moved by 1% of the time
where the time goes in v7:
time: 48.5 us; the launch traced here: 48.3 us
  blocking collectives  39.3 us (81%)
  starting transfers between devices  3.67 us (8%)
  Pallas kernels  3.62 us (7%)
  waiting for transfers between devices  0.99 us (2%)
  between operations  0.65 us (1%)
    all_to_all x1, blocking collectives, per_device(): recv = lax.all_to_all(send, 'ctx', 0, 0, axis_index_groups=ring, tiled=True)  15.4 us
    all_to_all x1, blocking collectives, per_device(): lax.all_to_all(spread(back, peers // 2, groups_here, own), 'ch', 0, 0, ax...  14.3 us
    all_to_all x1, blocking collectives, per_device(): lax.all_to_all(gradients(recv), 'ctx', 0, 0, axis_index_groups=ring, tile...  9.67 us
    ppermute x1, starting transfers between devices, per_device(): theirs = lax.ppermute(mine, 'ch', [(k, k ^ 1) for k in range(peers)])  3.67 us
    pallas_call x1, Pallas kernels, gradients(): pl.pallas_call(gradients_kernel, out_shape=pltpu.VMEM((blocks, span + 8,...  1.71 us
    pallas_call x1, Pallas kernels, pack(): pl.pallas_call(pack_kernel, out_shape=pltpu.VMEM((blocks, 2 * span + 8, 1...  1.08 us
    ppermute x1, waiting for transfers between devices, per_device(): theirs = lax.ppermute(mine, 'ch', [(k, k ^ 1) for k in range(peers)])  0.99 us
  transfers between devices with their start and end apart: 1, of which 1 were waited for; matrix products, arithmetic and copies ran while one was open for 0% of the time, Pallas kernels for 0%

profile of v7, /device:TPU:1, one launch (start us, length us, event | category | flops | bytes accessed | tf_op | source)
XLA Modules:
  0.0 48.3 jit_solution(4822060904961394571)
XLA Ops:
  0.6 1.1 %pack.1 = bf16[8,264,128]{2,1,0:T(8,128)(2,1)S(1)} custom-call(bf16[8,128,128]{2,1,0:T(8,128)(2,1)} %bitcast.16, bf16[8,128,128]{2,1,0:T(8,128)(2,1)} %bitcast.17, bf16[128,512]{1,0:T(8,128)(2,1)} %filter_ref.1), custom_call_target="tpu_custom_call" | custom-call | tf_op jit(solution)/shard_map/pack/pallas_call | solution.py:50
  1.7 15.4 %all_to_all.15.recv_ref = bf16[8,264,128]{2,1,0:T(8,128)(2,1)S(1)} all-to-all(bf16[8,264,128]{2,1,0:T(8,128)(2,1)S(1)} %pack.1), channel_id=1, replica_groups={{192,224,128,160,64,96,0,32},{193,225,129,161,65,97,1,33},{194,226,130,..., dimensions={0} | all-to-all | bytes 1081344 | tf_op jit(solution)/shard_map/all_to_all | solution.py:280
  17.1 1.7 %gradients.1 = bf16[8,136,128]{2,1,0:T(8,128)(2,1)S(1)} custom-call(bf16[8,264,128]{2,1,0:T(8,128)(2,1)S(1)} %all_to_all.15.recv_ref), custom_call_target="tpu_custom_call" | custom-call | tf_op jit(solution)/shard_map/gradients/pallas_call | solution.py:191
  18.8 9.7 %all_to_all.16.back_ref = bf16[8,136,128]{2,1,0:T(8,128)(2,1)S(1)} all-to-all(bf16[8,136,128]{2,1,0:T(8,128)(2,1)S(1)} %gradients.1), channel_id=1, replica_groups={{192,224,128,160,64,96,0,32},{193,225,129,161,65,97,1,33},{194,226,130,..., dimensions={0} | all-to-all | bytes 557056 | tf_op jit(solution)/shard_map/all_to_all | solution.py:281
  28.5 14.3 %all_to_all.17.mine_ref = f32[16,4,512]{2,1,0:T(4,128)S(1)} all-to-all(f32[16,4,512]{2,1,0:T(4,128)S(1)} %spread.1), channel_id=1, replica_groups={{8,10,12,14,0,2,4,6,24,26,28,30,16,18,20,22},{9,11,13,15,1,3,5,7,25,27,..., dimensions={0} | all-to-all | bytes 262144 | tf_op jit(solution)/shard_map/all_to_all | solution.py:284
  42.8 3.7 %collective-permute-start = (f32[16,4,512]{2,1,0:T(4,128)S(1)}, f32[16,4,512]{2,1,0:T(4,128)S(1)}, u32[]{:S(2)}, u32[]{:S(2)}) collective-permute-start(f32[16,4,512]{2,1,0:T(4,128)S(1)} %all_to_all.17.mine_ref), channel_id=1, source_target_pairs={{0,1},{1,0},{2,3},{3,2},{4,5},{5,4},{6,7},{7,6},{8,9},{9,8},{10,11... | collective-permute-start | bytes 393224 | tf_op jit(solution)/shard_map/ppermute | solution.py:294
  46.5 1.0 %collective-permute-done.theirs_ref = f32[16,4,512]{2,1,0:T(4,128)S(1)} collective-permute-done((f32[16,4,512]{2,1,0:T(4,128)S(1)}, f32[16,4,512]{2,1,0:T(4,128)S(1)}, u32[]{:S(2)}, u32[]{:S(2)}) %collective-permute-start) | collective-permute-done | bytes 131104 | tf_op jit(solution)/shard_map/ppermute | solution.py:294
  47.5 0.8 %finish.1 = (bf16[8,128,128]{2,1,0:T(8,128)(2,1)}, f32[16,8,512]{2,1,0:T(8,128)}) custom-call(bf16[8,136,128]{2,1,0:T(8,128)(2,1)S(1)} %all_to_all.16.back_ref, f32[16,4,512]{2,1,0:T(4,128)S(1)} %all_to_all.17.mine_ref, f32[16,4,512]{2,1,0:T(4,128)S(1)} %collective-permute-done.theirs_ref), custom_call_target="tpu_custom_call" | custom-call | tf_op jit(solution)/shard_map/finish/pallas_call | solution.py:258
  (1 shorter events, 0.0 us)
Async XLA Ops:
  42.8 4.7 %collective-permute-start = (f32[16,4,512]{2,1,0:T(4,128)S(1)}, f32[16,4,512]{2,1,0:T(4,128)S(1)}, u32[]{:S(2)}, u32[]{:S(2)}) collective-permute-start(f32[16,4,512]{2,1,0:T(4,128)S(1)} %all_to_all.17.mine_ref), channel_id=1, source_target_pairs={{0,1},{1,0},{2,3},{3,2},{4,5},{5,4},{6,7},{7,6},{8,9},{9,8},{10,11... | collective-permute-start | bytes 393224 | tf_op jit(solution)/shard_map/ppermute | solution.py:294
